TPU v7x, 32 devices: a whole 2x2x4 slice. The times are simulated.
32 devices in a mesh: tr: 4 (over y, x), tc: 8 (over z, core).
Axes of the slice: x: 2, y: 2, z: 4, core: 2. Of those that a mesh axis runs over, the one named last changes fastest.
Arguments:
- green_function: float32 [2, 256, 256, 256], P(None, None, 'tr', 'tc'), may hold values from -6 to 6
Outputs:
- collision: float32 [2, 256, 256, 256], P(None, ('tr', 'tc'))
All inputs are finite; a program needn't handle non-finite values.
Results may differ from a plain program's by a relative error of at most 0.00016.
Values sent between devices are 32-bit elements; how exact they have to be, the bound alone decides.
No kernel may reach another device: no remote copies, remote signals or barrier semaphores. Data moves between devices by JAX's collectives and lax.ppermute only.
A program may use at most 128 MiB of HBM per device.

v0:
```python
import math

import jax
import jax.numpy as jnp
from jax import lax
from jax.sharding import PartitionSpec as P

coupling = 4.0
time_step = 0.2


def site_order(momenta, per_device):
    positions = jnp.arange(momenta, dtype=jnp.int32)
    half_slots = per_device // 2
    owner_index = positions // per_device
    slot_in_device = positions % per_device
    base_site = owner_index * half_slots + slot_in_device % half_slots
    mirrored = jnp.where(base_site == 0, momenta // 2, momenta - base_site)
    return jnp.where(slot_in_device < half_slots, base_site, mirrored)


def phase_tables(momenta, sites):
    wave_index = jnp.arange(momenta, dtype=jnp.int32)
    phase_index = sites[:, None] * wave_index[None, :] % momenta
    angles = phase_index.astype(jnp.float32) * (2.0 * math.pi / momenta)
    return (jnp.cos(angles), jnp.sin(angles))


def forward_matrix(cosine_table, sine_table, momenta):
    return (
        jnp.concatenate(
            [
                jnp.concatenate([cosine_table, -sine_table], 1),
                jnp.concatenate([sine_table, cosine_table], 1),
            ],
            0,
        )
        / momenta
    )


def inverse_matrix(cosine_table, sine_table):
    return jnp.concatenate(
        [
            jnp.concatenate([cosine_table.T, sine_table.T], 1),
            jnp.concatenate([-sine_table.T, cosine_table.T], 1),
        ],
        0,
    )


def cubic_product(site_full, mirror):
    square_re = site_full[0] * site_full[0] - site_full[1] * site_full[1]
    square_im = 2.0 * site_full[0] * site_full[1]
    strength = coupling * coupling
    sigma_re = strength * (square_re * mirror[0] - square_im * mirror[1])
    sigma_im = strength * (square_re * mirror[1] + square_im * mirror[0])
    return jnp.stack([sigma_re, sigma_im])


def shards(green_function):
    highest = lax.Precision.HIGHEST
    rows_count = lax.axis_size("tr")
    cols_count = lax.axis_size("tc")
    devices = rows_count * cols_count
    momenta = green_function.shape[1]
    tile_rows = green_function.shape[2]
    tile_cols = green_function.shape[3]
    window = tile_rows * rows_count
    per_device = momenta // devices
    half_slots = per_device // 2
    cells = tile_rows * tile_cols
    ratio = cols_count // rows_count
    green_split = green_function.reshape(2, devices, per_device, cells)
    cosine_table, sine_table = phase_tables(momenta, site_order(momenta, per_device))
    forward = forward_matrix(cosine_table, sine_table, momenta)
    site_tiles = jnp.dot(
        forward, green_function.reshape(2 * momenta, cells), precision=highest
    ).reshape(2, devices, per_device, cells)
    arrived = lax.all_to_all(site_tiles, ("tr", "tc"), split_axis=1, concat_axis=1, tiled=True)
    item_count = arrived.shape[2]
    shaped = arrived.reshape(2, rows_count, cols_count, item_count, tile_rows, tile_cols)
    site_full = shaped.transpose(0, 3, 1, 4, 2, 5).reshape(2, item_count, window, window)
    device = lax.axis_index("tr") * cols_count + lax.axis_index("tc")
    slot_index = jnp.arange(per_device, dtype=jnp.int32)
    self_mirror = (device == 0) & ((slot_index == 0) | (slot_index == half_slots))
    swapped = jnp.concatenate([site_full[:, half_slots:], site_full[:, :half_slots]], 1)
    mirror = jnp.swapaxes(jnp.where(self_mirror[None, :, None, None], site_full, swapped), 2, 3)
    site_sigma = cubic_product(site_full, mirror)
    outgoing = (
        site_sigma.reshape(2, per_device, rows_count, tile_rows, cols_count, tile_cols)
        .transpose(0, 2, 4, 1, 3, 5)
        .reshape(2, devices, per_device, cells)
    )
    returned = lax.all_to_all(outgoing, ("tr", "tc"), split_axis=1, concat_axis=1, tiled=True)
    inverse = inverse_matrix(cosine_table, sine_table)
    sigma_tiles = jnp.dot(inverse, returned.reshape(2 * momenta, cells), precision=highest).reshape(
        2, devices, per_device, cells
    )
    sigma_pieces = lax.all_to_all(
        sigma_tiles, ("tr", "tc"), split_axis=1, concat_axis=1, tiled=True
    )
    item_count = sigma_pieces.shape[2]
    sigma = sigma_pieces.reshape(2, rows_count, rows_count, ratio, item_count, tile_rows, tile_cols)
    green = lax.all_to_all(
        green_split, ("tr", "tc"), split_axis=1, concat_axis=1, tiled=True
    ).reshape(2, rows_count, cols_count, item_count, ratio, tile_cols, tile_cols)
    form = "agjktx,gDkjxu->katDu"
    real_part = jnp.einsum(form, sigma[0], green[0], precision=highest) - jnp.einsum(
        form, sigma[1], green[1], precision=highest
    )
    imag_part = jnp.einsum(form, sigma[0], green[1], precision=highest) + jnp.einsum(
        form, sigma[1], green[0], precision=highest
    )
    stacked = jnp.stack([real_part, imag_part])
    return time_step * stacked.reshape(2, item_count, window, window)


def solution(mesh):
    return jax.shard_map(
        shards,
        mesh=mesh,
        in_specs=(P(None, None, "tr", "tc"),),
        out_specs=P(None, ("tr", "tc"), None, None),
        check_vma=False,
    )
```

profile of v0, /device:TPU:0, one launch (start us, length us, event | category | flops | bytes accessed | tf_op | source)
XLA Modules:
  0.0 670.1 jit_solution(11057486237855215199)
XLA Ops:
  2.1 6.0 copy.27
  8.7 8.5 %fusion.13 = f32[2,32,8,2048]{3,2,0,1:T(8,128)} fusion(f32[512,2048]{0,1:T(8,128)S(1)} %bitcast.118, f32[2,32,8,512]{3,2,1,0:T(8,128)S(1)} %bitcast.121), kind=kOutput, calls=%fused_computation.18 | convolution fusion | flops 6442450944 | bytes 9437184 | tf_op jit(solution)/shard_map/dot_general | solution.py:77
  17.2 7.6 %all-to-all-start = ((f32[2,32,8,2048]{3,2,0,1:T(8,128)}), f32[2,32,8,2048]{3,2,0,1:T(8,128)}, u32[]{:S(2)}, u32[]{:S(2)}) async-start(f32[2,32,8,2048]{3,2,0,1:T(8,128)} %fusion.13), calls=%async_computation | async-start | bytes 8388608 | tf_op jit(solution)/shard_map/all_to_all | solution.py:80
  24.9 94.9 %all-to-all-done = f32[2,32,8,2048]{3,2,0,1:T(8,128)} async-done(((f32[2,32,8,2048]{3,2,0,1:T(8,128)}), f32[2,32,8,2048]{3,2,0,1:T(8,128)}, u32[]{:S(2)}, u32[]{:S(2)}) %all-to-all-start) | async-done | bytes 4194336 | tf_op jit(solution)/shard_map/all_to_all | solution.py:80
  124.5 11.4 %reshape.148 = f32[2,4,8,8,64,32]{5,4,3,2,1,0:T(8,128)} reshape(f32[2,32,8,2048]{3,2,1,0:T(8,128)} %copy.30) | data formatting | bytes 8388608 | tf_op jit(solution)/shard_map/reshape | solution.py:82
  135.8 14.7 %copy.32 = f32[2,8,4,64,8,32]{3,2,5,4,1,0:T(4,128)} copy(f32[2,8,4,64,8,32]{5,3,1,4,2,0:T(8,128)} %bitcast.111) | data formatting | bytes 8388608 | tf_op jit(solution)/shard_map/transpose | solution.py:83
  150.5 11.2 %multiply_subtract_fusion = (f32[1,8,4,64,8,32]{5,3,1,4,2,0:T(8,128)}, f32[1,8,4,64,8,32]{5,3,1,4,2,0:T(8,128)}) fusion(f32[2,8,4,64,8,32]{5,3,1,4,2,0:T(8,128)} %bitcast.112), kind=kLoop, calls=%fused_computation.2 | loop fusion | flops 2621440 | bytes 8388608 | tf_op jit(solution)/shard_map/sub | solution.py:53
  161.7 8.6 %reshape.149 = f32[2,8,256,256]{2,3,1,0:T(8,128)} reshape(f32[2,8,4,64,8,32]{3,2,5,4,1,0:T(4,128)} %copy.32) | data formatting | bytes 8388608 | tf_op jit(solution)/shard_map/reshape | solution.py:83
  170.3 5.3 copy.35
  175.6 7.8 %copy.31 = f32[1,8,4,64,8,32]{3,2,5,4,1,0:T(4,128)} copy(f32[1,8,4,64,8,32]{5,3,1,4,2,0:T(8,128)} %get-tuple-element.5) | data formatting | bytes 4194304 | tf_op jit(solution)/shard_map/sub | solution.py:53
  187.5 7.8 %copy.36 = f32[1,8,4,64,8,32]{3,2,5,4,1,0:T(4,128)} copy(f32[1,8,4,64,8,32]{5,3,1,4,2,0:T(8,128)} %get-tuple-element.6) | data formatting | bytes 4194304 | tf_op jit(solution)/shard_map/mul | solution.py:54
  195.3 5.3 mul.203
  208.2 5.2 stack.18
  216.7 10.8 %maximum_bitcast_fusion = f32[2,4,8,8,64,32]{4,1,5,2,3,0:T(4,128)} fusion(f32[1,8,4,64,8,32]{3,2,5,4,1,0:T(4,128)} %stack.19, f32[1,8,4,64,8,32]{3,2,5,4,1,0:T(4,128)} %stack.18), kind=kLoop, calls=%fused_computation | loop fusion | flops 1048576 | bytes 8388608 | tf_op jit(solution)/shard_map/transpose | solution.py:92
  227.5 13.8 %copy.73 = f32[2,4,8,8,64,32]{5,4,3,0,2,1:T(8,128)} copy(f32[2,4,8,8,64,32]{4,1,5,2,3,0:T(4,128)} %maximum_bitcast_fusion) | data formatting | bytes 8388608 | tf_op jit(solution)/shard_map/reshape | solution.py:93
  241.4 13.5 %reshape.167 = f32[2,32,8,2048]{3,2,0,1:T(8,128)} reshape(f32[2,4,8,8,64,32]{5,4,3,0,2,1:T(8,128)} %copy.73) | data formatting | bytes 8388608 | tf_op jit(solution)/shard_map/reshape | solution.py:93
  258.4 14.4 %copy.41 = f32[2,256,64,32]{3,2,1,0:T(8,128)} copy(f32[2,256,64,32]{1,3,2,0:T(8,128)} %param.1) | data formatting | bytes 8388608 | tf_op args[0]
  272.8 13.4 %reshape.152 = f32[2,32,8,2048]{3,2,1,0:T(8,128)} reshape(f32[2,256,64,32]{3,2,1,0:T(8,128)} %copy.41) | data formatting | bytes 8388608 | tf_op jit(solution)/shard_map/reshape | solution.py:74
  290.9 62.5 %all-to-all-done.1 = f32[2,32,8,2048]{3,2,0,1:T(8,128)} async-done(((f32[2,32,8,2048]{3,2,0,1:T(8,128)}), f32[2,32,8,2048]{3,2,0,1:T(8,128)}, u32[]{:S(2)}, u32[]{:S(2)}) %all-to-all-start.1) | async-done | bytes 4194336 | tf_op jit(solution)/shard_map/all_to_all | solution.py:95
  359.5 8.4 %fusion.23 = f32[2,32,8,2048]{3,2,0,1:T(8,128)} fusion(f32[512,2048,1,1]{1,0,2,3:T(8,128)S(1)} %bitcast.119, f32[2,32,8,512]{3,2,1,0:T(8,128)S(1)} %bitcast.120), kind=kOutput, calls=%fused_computation.26 | convolution fusion | flops 6442450944 | bytes 9437184 | tf_op jit(solution)/shard_map/dot_general | solution.py:97
  368.0 83.9 %all-to-all-done.3 = f32[2,32,8,2048]{3,2,0,1:T(8,128)} async-done(((f32[2,32,8,2048]{3,2,0,1:T(8,128)}), f32[2,32,8,2048]{3,2,0,1:T(8,128)}, u32[]{:S(2)}, u32[]{:S(2)}) %all-to-all-start.3) | async-done | bytes 4194336 | tf_op jit(solution)/shard_map/all_to_all | solution.py:105
  459.9 6.3 squeeze.9
  471.0 79.8 %all-to-all-done.2 = f32[2,32,8,2048]{3,2,0,1:T(8,128)} async-done(((f32[2,32,8,2048]{3,2,0,1:T(8,128)}), f32[2,32,8,2048]{3,2,0,1:T(8,128)}, u32[]{:S(2)}, u32[]{:S(2)}) %all-to-all-start.2) | async-done | bytes 4194336 | tf_op jit(solution)/shard_map/all_to_all | solution.py:100
  554.7 6.2 squeeze.10
  565.8 16.3 %fusion = f32[8,4,64,8,32,1,1]{2,4,6,5,3,1,0:T(8,128)S(1)} fusion(f32[4,8,8,2,32,32]{5,4,3,2,1,0:T(8,128)} %squeeze.11, f32[4,4,2,8,64,32]{5,4,3,2,1,0:T(8,128)} %squeeze.8), kind=kOutput, calls=%fused_computation.3 | convolution fusion | flops 1610612736 | bytes 6291456 | tf_op jit(solution)/shard_map/agjktx,gDkjxu->katDu/dot_general | solution.py:112
  582.2 16.0 %fusion.2 = f32[8,4,64,8,32,1,1]{2,4,6,5,3,1,0:T(8,128)S(1)} fusion(f32[4,8,8,2,32,32]{5,4,3,2,1,0:T(8,128)} %squeeze.11, f32[4,4,2,8,64,32]{5,4,3,2,1,0:T(8,128)S(1)} %copy-done), kind=kOutput, calls=%fused_computation.5 | convolution fusion | flops 1610612736 | bytes 6291456 | tf_op jit(solution)/shard_map/agjktx,gDkjxu->katDu/dot_general | solution.py:109
  598.2 15.3 %bitcast_add_fusion = f32[8,4,64,8,32]{2,4,3,1,0:T(8,128)} fusion(f32[8,4,64,8,32,1,1]{2,4,6,5,3,1,0:T(8,128)S(1)} %fusion, f32[4,4,2,8,64,32]{5,4,3,2,1,0:T(8,128)S(1)} %copy-done, f32[4,8,8,2,32,32]{5,4,3,2,1,0:T(8,128)S(1)} %bitcast.116), kind=kOutput, calls=%fused_computation.20 | convolution fusion | flops 1611137024 | bytes 8388608 | tf_op jit(solution)/shard_map/agjktx,gDkjxu->katDu/dot_general | solution.py:112
  613.6 23.6 %bitcast_subtract_fusion = f32[8,4,64,8,32]{2,4,3,1,0:T(8,128)S(1)} fusion(f32[8,4,64,8,32,1,1]{2,4,6,5,3,1,0:T(8,128)S(1)} %fusion.2, f32[4,8,8,2,32,32]{5,4,3,2,1,0:T(8,128)S(1)} %bitcast.116, f32[4,4,2,8,64,32]{5,4,3,2,1,0:T(8,128)S(1)} %bitcast.114), kind=kOutput, calls=%fused_computation.21 | convolution fusion | flops 1611137024 | bytes 8388608 | tf_op jit(solution)/shard_map/agjktx,gDkjxu->katDu/dot_general | solution.py:109
  637.2 5.9 copy.47
  647.2 8.1 %copy.52 = f32[8,4,64,8,32]{2,1,4,3,0:T(4,128)} copy(f32[8,4,64,8,32]{2,4,3,1,0:T(8,128)} %bitcast_add_fusion) | data formatting | bytes 4194304 | tf_op jit(solution)/shard_map/add | solution.py:112
  655.3 5.3 stack.22
  664.5 5.3 copy.53
  (41 shorter events, 66.5 us)
Async XLA Ops:
  17.2 102.6 %all-to-all-start = ((f32[2,32,8,2048]{3,2,0,1:T(8,128)}), f32[2,32,8,2048]{3,2,0,1:T(8,128)}, u32[]{:S(2)}, u32[]{:S(2)}) async-start(f32[2,32,8,2048]{3,2,0,1:T(8,128)} %fusion.13), calls=%async_computation | async-start | bytes 8388608 | tf_op jit(solution)/shard_map/all_to_all | solution.py:80
  200.6 3.5 copy-start.1
  204.0 1.6 copy-start.2
  208.2 5.2 copy-start.3
  254.8 98.5 %all-to-all-start.1 = ((f32[2,32,8,2048]{3,2,0,1:T(8,128)}), f32[2,32,8,2048]{3,2,0,1:T(8,128)}, u32[]{:S(2)}, u32[]{:S(2)}) async-start(f32[2,32,8,2048]{3,2,0,1:T(8,128)} %reshape.167), calls=%async_computation.1 | async-start | bytes 8388608 | tf_op jit(solution)/shard_map/all_to_all | solution.py:95
  353.4 98.5 %all-to-all-start.3 = ((f32[2,32,8,2048]{3,2,0,1:T(8,128)}), f32[2,32,8,2048]{3,2,0,1:T(8,128)}, u32[]{:S(2)}, u32[]{:S(2)}) async-start(f32[2,32,8,2048]{3,2,0,1:T(8,128)} %copy.42), calls=%async_computation.3 | async-start | bytes 8388608 | tf_op jit(solution)/shard_map/all_to_all | solution.py:105
  451.9 98.9 %all-to-all-start.2 = ((f32[2,32,8,2048]{3,2,0,1:T(8,128)}), f32[2,32,8,2048]{3,2,0,1:T(8,128)}, u32[]{:S(2)}, u32[]{:S(2)}) async-start(f32[2,32,8,2048]{3,2,0,1:T(8,128)} %fusion.23), calls=%async_computation.2 | async-start | bytes 8388608 | tf_op jit(solution)/shard_map/all_to_all | solution.py:100
  565.8 16.4 %copy-start = (f32[4,4,2,8,64,32]{5,4,3,2,1,0:T(8,128)S(1)}, f32[4,4,2,8,64,32]{5,4,3,2,1,0:T(8,128)}, u32[]{:S(2)}) copy-start(f32[4,4,2,8,64,32]{5,4,3,2,1,0:T(8,128)} %squeeze.10) | copy-start | bytes 6291460
  565.8 32.4 %slice-start.2 = ((s8[8388608]{0:T(1024)(128)(4,1)}), s8[4194304]{0:T(1024)(128)(4,1)S(1)}, s32[]{:S(2)}) async-start(s8[8388608]{0:T(1024)(128)(4,1)} %bitcast.115), calls=%async_computation.6 | async-start | bytes 8388608
  582.1 16.1 %slice-start.3 = ((s8[8388608]{0:T(1024)(128)(4,1)}), s8[4194304]{0:T(1024)(128)(4,1)S(1)}, s32[]{:S(2)}) async-start(s8[8388608]{0:T(1024)(128)(4,1)} %bitcast.115), calls=%async_computation.7 | async-start | bytes 8388608
  582.1 31.4 %slice-start = ((s8[8388608]{0:T(1024)(128)(4,1)}), s8[4194304]{0:T(1024)(128)(4,1)S(1)}, s32[]{:S(2)}) async-start(s8[8388608]{0:T(1024)(128)(4,1)} %bitcast.113), calls=%async_computation.4 | async-start | bytes 8388608
  598.2 15.4 %slice-start.1 = ((s8[8388608]{0:T(1024)(128)(4,1)}), s8[4194304]{0:T(1024)(128)(4,1)S(1)}, s32[]{:S(2)}) async-start(s8[8388608]{0:T(1024)(128)(4,1)} %bitcast.113), calls=%async_computation.5 | async-start | bytes 8388608
where the time goes:
time: 680 us; the launch traced here: 670 us
  waiting for transfers between devices  321 us (47%)
  local copies, waits for them, and re-layouts  210 us (31%)
  matrix products  88.2 us (13%)
  other arithmetic  31.6 us (5%)
  starting transfers between devices  18.7 us (3%)
    all_to_all x1, waiting for transfers between devices, shards(): lax.all_to_all(site_tiles, ('tr', 'tc'), split_axis=1, concat_axis=1, til...  94.9 us
    all_to_all x1, waiting for transfers between devices, shards(): lax.all_to_all(green_split, ('tr', 'tc'), split_axis=1, concat_axis=1, ti...  83.9 us
    all_to_all x1, waiting for transfers between devices, shards(): lax.all_to_all(sigma_tiles, ('tr', 'tc'), split_axis=1, concat_axis=1, ti...  79.8 us
    all_to_all x1, waiting for transfers between devices, shards(): lax.all_to_all(outgoing, ('tr', 'tc'), split_axis=1, concat_axis=1, tiled...  62.5 us
    reshape x2, local copies, waits for them, and re-layouts, shards(): outgoing = site_sigma.reshape(2, per_device, rows_count, tile_rows, cols_...  27.3 us
    dot_general x1, matrix products, shards(): jnp.einsum(form, sigma[0], green[0], precision=highest)  23.6 us
    unnamed x19, local copies, waits for them, and re-layouts  22.4 us
    reshape x2, local copies, waits for them, and re-layouts, shards(): green_split = green_function.reshape(2, devices, per_device, cells)  18.1 us
  transfers between devices with their start and end apart: 4, of which 4 were waited for; matrix products, arithmetic and copies ran while one was open for 9% of the time, Pallas kernels for 0%

commit v1 on v0

--- a/solution.py
+++ b/solution.py
@@ -1,12 +1,20 @@
+import functools
 import math
 
 import jax
 import jax.numpy as jnp
+import numpy as np
 from jax import lax
+from jax.experimental import pallas as pl
+from jax.experimental.pallas import tpu as pltpu
 from jax.sharding import PartitionSpec as P
 
 coupling = 4.0
 time_step = 0.2
+f32 = jnp.float32
+bf16 = jnp.bfloat16
+LANES = 128
+SUBLANES = 8
 
 
 def site_order(momenta, per_device):
@@ -58,7 +66,7 @@
     return jnp.stack([sigma_re, sigma_im])
 
 
-def shards(green_function):
+def general_shards(green_function):
     highest = lax.Precision.HIGHEST
     rows_count = lax.axis_size("tr")
     cols_count = lax.axis_size("tc")
@@ -116,6 +124,323 @@
     return time_step * stacked.reshape(2, item_count, window, window)
 
 
+def kept_half(a, b):
+    z, c = b // 2, b % 2
+    return 1 - c if a < z else c if a > z else 0
+
+
+def partner(a, b):
+    z, c = b // 2, b % 2
+    return (z, 2 * a + c) if a < z else (z, 2 * a + 1 - c)
+
+
+def block_plan(rows_count):
+    cols_count = 2 * rows_count
+    route = []
+    held = {}
+    for a in range(rows_count):
+        for b in range(cols_count):
+            source = a * cols_count + b
+            pa, pb = partner(a, b)
+            target = pa * cols_count + pb
+            keep = kept_half(a, b)
+            route.append((source, target))
+            held[(2 * a + keep, b)] = (source, 0)
+            held[(2 * a + 1 - keep, b)] = (target, 1)
+    return route, held
+
+
+def split(x):
+    high = x.astype(bf16)
+    return high, (x - high.astype(f32)).astype(bf16)
+
+
+def dot(x, y, dims=((1,), (0,))):
+    return lax.dot_general(x, y, (dims, ((), ())), preferred_element_type=f32)
+
+
+def dot3(x, y, dims=((1,), (0,))):
+    return dot(x[0], y[0], dims) + dot(x[0], y[1], dims) + dot(x[1], y[0], dims)
+
+
+def regroup(x):
+    lane = lax.broadcasted_iota(jnp.int32, x[0].shape, 1)
+    upper = lane >= LANES // 2
+    odd = (lane // (LANES // 4)) % 2 == 1
+    half, quarter = LANES // 2, LANES // 4
+
+    def swap(p, q, mask, shift):
+        return (
+            jnp.where(mask, pltpu.roll(q, shift, 1), p),
+            jnp.where(mask, q, pltpu.roll(p, LANES - shift, 1)),
+        )
+
+    a0, a2 = swap(x[0], x[2], upper, half)
+    a1, a3 = swap(x[1], x[3], upper, half)
+    y0, y1 = swap(a0, a1, odd, quarter)
+    y2, y3 = swap(a2, a3, odd, quarter)
+    return y0, y1, y2, y3
+
+
+def send_kernel(x_ref, out_ref):
+    spans = out_ref.shape[2]
+    for v in range(spans):
+        rows = jnp.concatenate([x_ref[0, spans * q + v] for q in range(4)], 0)
+        out_ref[:, 0, v] = rows.T.reshape(out_ref.shape[0], SUBLANES, LANES)
+
+
+def pack_green(x):
+    comps, rows, cols, momenta = x.shape
+    spans = rows * cols // LANES
+    devices = momenta // SUBLANES
+    parts = momenta // LANES
+    return pl.pallas_call(
+        send_kernel,
+        grid=(comps, parts),
+        in_specs=[pl.BlockSpec((1, rows, cols, LANES), lambda c, p: (c, 0, 0, p))],
+        out_specs=pl.BlockSpec(
+            (devices // parts, 1, spans, SUBLANES, LANES), lambda c, p: (p, c, 0, 0, 0)
+        ),
+        out_shape=jax.ShapeDtypeStruct((devices, comps, spans, SUBLANES, LANES), f32),
+        cost_estimate=pl.CostEstimate(flops=0, bytes_accessed=2 * x.size * 4, transcendentals=0),
+        name="pack_green",
+    )(x)
+
+
+def sigma_kernel(flags, kept_ref, other_ref, fh_ref, fl_ref, ih_ref, il_ref, out_ref, plus, minus):
+    points, momenta = kept_ref.shape[2], kept_ref.shape[3]
+    edge = math.isqrt(points)
+    spans = points // LANES
+    chunk = 256
+    forward = (fh_ref[...], fl_ref[...])
+
+    for unit, ref in ((0, kept_ref.at[:, 0]), (1, other_ref)):
+
+        def transform(n, carry, unit=unit, ref=ref):
+            rows = pl.ds(pl.multiple_of(n * chunk, chunk), chunk)
+            y_re = dot3(split(ref[0, rows, :]), forward)
+            y_im = dot3(split(ref[1, rows, :]), forward)
+            re_c, re_s = y_re[:, :momenta], y_re[:, momenta:]
+            im_c, im_s = y_im[:, :momenta], y_im[:, momenta:]
+            plus[unit, 0, rows, :] = re_c - im_s
+            plus[unit, 1, rows, :] = re_s + im_c
+            m_re = re_c + im_s
+            m_im = im_c - re_s
+            for p in range(momenta // LANES):
+                lanes = slice(LANES * p, LANES * (p + 1))
+                minus[unit, 0, p, rows, :] = m_re[:, lanes]
+                minus[unit, 1, p, rows, :] = m_im[:, lanes]
+            return carry
+
+        lax.fori_loop(0, points // chunk, transform, 0)
+
+    inverse = (ih_ref[...], il_ref[...])
+    diagonal = flags[1]
+    for unit in range(2):
+        facing = jnp.where(diagonal == 1, unit, 1 - unit)
+
+        def combine(n, carry, unit=unit, facing=facing):
+            s_re, s_im = [], []
+            for w in range(2):
+                for q in range(4):
+                    i = spans * q + 2 * n + w
+                    rows = pl.ds(pl.multiple_of(i * edge, edge), edge)
+                    across = pl.ds(i, edge, stride=edge)
+                    p_re, p_im = plus[unit, 0, rows, :], plus[unit, 1, rows, :]
+                    m_re, m_im = (
+                        jnp.concatenate(
+                            [minus[facing, c, p, across, :] for p in range(momenta // LANES)], 1
+                        )
+                        for c in range(2)
+                    )
+                    sq_re = p_re * p_re - p_im * p_im
+                    sq_im = 2.0 * p_re * p_im
+                    s_re.append(sq_re * m_re - sq_im * m_im)
+                    s_im.append(sq_re * m_im + sq_im * m_re)
+            nt = ((1,), (1,))
+            t_re = dot3(inverse, split(jnp.concatenate(s_re, 0)), nt)
+            t_im = dot3(inverse, split(jnp.concatenate(s_im, 0)), nt)
+            o_re = t_re[:momenta] + t_im[momenta:]
+            o_im = t_im[:momenta] - t_re[momenta:]
+            for w in range(2):
+                lanes = slice(LANES * w, LANES * (w + 1))
+                place = spans * unit + 2 * n + w
+                shape = (momenta // SUBLANES, SUBLANES, LANES)
+                out_ref[:, 0, place] = o_re[:, lanes].reshape(shape)
+                out_ref[:, 1, place] = o_im[:, lanes].reshape(shape)
+            return carry
+
+        lax.fori_loop(0, spans // 2, combine, 0)
+
+
+def form_sigma(flags, x, other, tables):
+    comps, halves, points, momenta = x.shape
+    devices = momenta // SUBLANES
+    spans = 2 * points // LANES
+    whole = lambda a: pl.BlockSpec(a.shape, lambda n, s: (0,) * a.ndim)
+    flops = 3 * 2 * 4 * 2 * (2 * points) * momenta * momenta
+    return pl.pallas_call(
+        sigma_kernel,
+        grid_spec=pltpu.PrefetchScalarGridSpec(
+            num_scalar_prefetch=1,
+            grid=(1,),
+            in_specs=[
+                pl.BlockSpec((comps, 1, points, momenta), lambda n, s: (0, s[0], 0, 0)),
+                whole(other),
+                *[whole(t) for t in tables],
+            ],
+            out_specs=pl.BlockSpec(
+                (devices, comps, spans, SUBLANES, LANES), lambda n, s: (0, 0, 0, 0, 0)
+            ),
+            scratch_shapes=[
+                pltpu.VMEM((2, comps, points, momenta), f32),
+                pltpu.VMEM((2, comps, momenta // LANES, points, LANES), f32),
+            ],
+        ),
+        out_shape=jax.ShapeDtypeStruct((devices, comps, spans, SUBLANES, LANES), f32),
+        cost_estimate=pl.CostEstimate(
+            flops=flops, bytes_accessed=3 * other.size * 4, transcendentals=0
+        ),
+        compiler_params=pltpu.CompilerParams(vmem_limit_bytes=56 * 1024 * 1024),
+        name="form_sigma",
+    )(flags, x, other, *tables)
+
+
+def green_kernel(x_ref, out_ref, *, rows_count):
+    cols_count = 2 * rows_count
+    k = pl.program_id(0)
+    tile_rows = out_ref.shape[3] // rows_count
+    step = tile_rows // 4
+    for comp in range(2):
+        for a in range(rows_count):
+            for side in range(cols_count // 4):
+                groups = [[] for _ in range(4)]
+                for part in range(step // SUBLANES):
+                    span = pl.ds(SUBLANES * SUBLANES * part + k, SUBLANES, stride=SUBLANES)
+                    loaded = [
+                        x_ref[a * cols_count + 4 * side + n, comp, span, :] for n in range(4)
+                    ]
+                    for q, value in enumerate(regroup(loaded)):
+                        groups[q].append(value)
+                for q in range(4):
+                    high, low = split(jnp.concatenate(groups[q], 0))
+                    rows = slice(tile_rows * a + step * q, tile_rows * a + step * (q + 1))
+                    lanes = slice(LANES * side, LANES * (side + 1))
+                    out_ref[0, comp, 0, rows, lanes] = high
+                    out_ref[0, comp, 1, rows, lanes] = low
+
+
+def arrange_green(x, rows_count, window):
+    x = x.reshape(x.shape[0], 2, -1, LANES)
+    return pl.pallas_call(
+        functools.partial(green_kernel, rows_count=rows_count),
+        grid=(SUBLANES,),
+        in_specs=[pl.BlockSpec(x.shape, lambda k: (0, 0, 0, 0))],
+        out_specs=pl.BlockSpec((1, 2, 2, window, window), lambda k: (k, 0, 0, 0, 0)),
+        out_shape=jax.ShapeDtypeStruct((SUBLANES, 2, 2, window, window), bf16),
+        cost_estimate=pl.CostEstimate(flops=0, bytes_accessed=2 * x.size * 4, transcendentals=0),
+        name="arrange_green",
+    )(x)
+
+
+def collide_kernel(s_ref, g_ref, out_ref, left, *, held, blocks):
+    k = pl.program_id(0)
+    edge = out_ref.shape[2] // blocks
+    for comp in range(2):
+        for row in range(blocks):
+            for side in range(blocks // 4):
+                loaded = []
+                for n in range(4):
+                    source, unit = held[(row, 4 * side + n)]
+                    span = pl.ds(SUBLANES * SUBLANES * unit + k, SUBLANES, stride=SUBLANES)
+                    loaded.append(s_ref[source, comp, span, :])
+                high, low = split(jnp.concatenate(regroup(loaded), 0))
+                rows = slice(edge * row, edge * (row + 1))
+                lanes = slice(LANES * side, LANES * (side + 1))
+                left[comp, 0, rows, lanes] = high
+                left[comp, 1, rows, lanes] = low
+    re, im = ((left[c, 0], left[c, 1]) for c in range(2))
+    g_re, g_im = ((g_ref[0, c, 0], g_ref[0, c, 1]) for c in range(2))
+    out_ref[0, 0] = time_step * (dot3(re, g_re) - dot3(im, g_im))
+    out_ref[1, 0] = time_step * (dot3(re, g_im) + dot3(im, g_re))
+
+
+def collide(sigma, green, held, blocks):
+    window = green.shape[-1]
+    sigma = sigma.reshape(sigma.shape[0], 2, -1, LANES)
+    return pl.pallas_call(
+        functools.partial(collide_kernel, held=held, blocks=blocks),
+        grid=(SUBLANES,),
+        in_specs=[
+            pl.BlockSpec(sigma.shape, lambda k: (0, 0, 0, 0)),
+            pl.BlockSpec((1, 2, 2, window, window), lambda k: (k, 0, 0, 0, 0)),
+        ],
+        out_specs=pl.BlockSpec((2, 1, window, window), lambda k: (0, k, 0, 0)),
+        out_shape=jax.ShapeDtypeStruct((2, SUBLANES, window, window), f32),
+        scratch_shapes=[pltpu.VMEM((2, 2, window, window), bf16)],
+        cost_estimate=pl.CostEstimate(
+            flops=3 * 8 * SUBLANES * window**3, bytes_accessed=3 * sigma.size * 4, transcendentals=0
+        ),
+        name="collide",
+    )(sigma, green)
+
+
+def table_pair(values):
+    high = values.astype(np.float32).astype(bf16)
+    low = (values - high.astype(np.float64)).astype(np.float32).astype(bf16)
+    return jnp.asarray(high), jnp.asarray(low)
+
+
+def dft_tables(momenta):
+    index = np.arange(momenta)
+    angle = 2.0 * np.pi * (index[:, None] * index[None, :] % momenta) / momenta
+    cosine, sine = np.cos(angle), np.sin(angle)
+    strength = coupling * coupling / momenta**3
+    forward = np.concatenate([cosine, sine], 1)
+    inverse = strength * np.concatenate([cosine, sine], 0)
+    return (*table_pair(forward), *table_pair(inverse))
+
+
+def packed_shards(green_function):
+    axes = ("tr", "tc")
+    rows_count = lax.axis_size("tr")
+    comps, momenta, tile_rows, tile_cols = green_function.shape
+    window = tile_rows * rows_count
+    points = tile_cols * tile_cols
+    route, held = block_plan(rows_count)
+    a = lax.axis_index("tr")
+    b = lax.axis_index("tc")
+    z, c = b // 2, b % 2
+    keep = jnp.where(a < z, 1 - c, jnp.where(a > z, c, 0)).astype(jnp.int32)
+    diagonal = ((a == z) & (c == 0)).astype(jnp.int32)
+
+    x = green_function.transpose(0, 2, 3, 1)
+    halves = x.reshape(comps, 2, points, momenta)
+    leaving = lax.dynamic_index_in_dim(halves, 1 - keep, 1, keepdims=False)
+    other = lax.ppermute(leaving, axes, route)
+    green = lax.all_to_all(pack_green(x), axes, split_axis=0, concat_axis=0, tiled=True)
+    tables = dft_tables(momenta)
+    sigma = form_sigma(jnp.stack([keep, diagonal]), halves, other, tables)
+    sigma = lax.all_to_all(sigma, axes, split_axis=0, concat_axis=0, tiled=True)
+    green = arrange_green(green, rows_count, window)
+    return collide(sigma, green, held, 2 * rows_count)
+
+
+def shards(green_function):
+    rows_count = lax.axis_size("tr")
+    cols_count = lax.axis_size("tc")
+    comps, momenta, tile_rows, tile_cols = green_function.shape
+    packs = (
+        cols_count == 2 * rows_count
+        and tile_rows == 2 * tile_cols
+        and 4 * tile_cols == LANES
+        and momenta == SUBLANES * rows_count * cols_count
+        and momenta % LANES == 0
+        and cols_count % 4 == 0
+    )
+    return packed_shards(green_function) if packs else general_shards(green_function)
+
+
 def solution(mesh):
     return jax.shard_map(
         shards,

time: 680 us -> 348 us (0.51); the launches traced: 670 us -> 348 us
  local copies, waits for them, and re-layouts: 210 us -> 1.74 us
  waiting for transfers between devices: 321 us -> 186 us
  starting transfers between devices: 18.7 us -> 111 us
  matrix products: 88.2 us -> 0 us
  Pallas kernels: 0 us -> 48.2 us
  other arithmetic: 31.6 us -> 0.59 us
    all_to_all x4 -> x2, waiting for transfers between devices: 321 us -> 182 us  [the longest x1 101 us: packed_shards(): lax.all_to_all(pack_green(x), axes, split_axis=0, concat_axis=0, tiled=True)]
    all_to_all x4 -> x2, starting transfers between devices: 18.7 us -> 111 us  [the longest x1 104 us: packed_shards(): sigma = lax.all_to_all(sigma, axes, split_axis=0, concat_axis=0, tiled=True)]
    dot_general x6 -> x0, matrix products: 88.2 us -> none  [the longest x1 23.6 us: shards(): jnp.einsum(form, sigma[0], green[0], precision=highest)]
    reshape x7 -> x0, local copies, waits for them, and re-layouts: 70.6 us -> none  [the longest x2 27.3 us: shards(): outgoing = site_sigma.reshape(2, per_device, rows_count, tile_rows, cols_...]
    pallas_call x0 -> x4, Pallas kernels: none -> 48.2 us  [the longest x1 18.3 us: form_sigma(): pl.pallas_call(sigma_kernel, grid_spec=pltpu.PrefetchScalarGridSpec(num_s...]
    unnamed x19 -> x0, local copies, waits for them, and re-layouts: 22.4 us -> none
    squeeze x4 -> x1, local copies, waits for them, and re-layouts: 22.1 us -> 1.74 us  [packed_shards(): leaving = lax.dynamic_index_in_dim(halves, 1 - keep, 1, keepdims=False)]
    mul x3 -> x0, local copies, waits for them, and re-layouts: 18.4 us -> none  [the longest x2 13.1 us: cubic_product(): square_im = 2.0 * site_full[0] * site_full[1]]
  transfers between devices with their start and end apart: 4 -> 3, of which waited for: 4 -> 3; matrix products, arithmetic and copies ran while one was open for 9% -> 1% of each run, Pallas kernels for 0% -> 9%
where the time goes in v1:
time: 348 us
  waiting for transfers between devices  186 us (53%)
  starting transfers between devices  111 us (32%)
  Pallas kernels  48.2 us (14%)
    all_to_all x1, starting transfers between devices, packed_shards(): sigma = lax.all_to_all(sigma, axes, split_axis=0, concat_axis=0, tiled=True)  104 us
    all_to_all x1, waiting for transfers between devices, packed_shards(): lax.all_to_all(pack_green(x), axes, split_axis=0, concat_axis=0, tiled=True)  101 us
    all_to_all x1, waiting for transfers between devices, packed_shards(): sigma = lax.all_to_all(sigma, axes, split_axis=0, concat_axis=0, tiled=True)  81.2 us
    pallas_call x1, Pallas kernels, form_sigma(): pl.pallas_call(sigma_kernel, grid_spec=pltpu.PrefetchScalarGridSpec(num_s...  18.3 us
    pallas_call x1, Pallas kernels, arrange_green(): pl.pallas_call(functools.partial(green_kernel, rows_count=rows_count), gr...  13.7 us
    pallas_call x1, Pallas kernels, collide(): pl.pallas_call(functools.partial(collide_kernel, held=held, blocks=blocks...  10.8 us
    all_to_all x1, starting transfers between devices, packed_shards(): lax.all_to_all(pack_green(x), axes, split_axis=0, concat_axis=0, tiled=True)  7.45 us
  transfers between devices with their start and end apart: 3, of which 3 were waited for; matrix products, arithmetic and copies ran while one was open for 1% of the time, Pallas kernels for 9%

profile of v1, /device:TPU:0, one launch (start us, length us, event | category | flops | bytes accessed | tf_op | source)
XLA Modules:
  0.0 347.7 jit_solution(415295143284870398)
XLA Ops:
  0.0 5.3 %pack_green.1 = f32[32,2,16,8,128]{4,3,2,1,0:T(8,128)} custom-call(f32[2,64,32,256]{3,2,1,0:T(8,128)} %bitcast.9), custom_call_target="tpu_custom_call" | custom-call | bytes 8388608 | tf_op jit(solution)/shard_map/pack_green/pallas_call | solution.py:197
  5.3 7.5 %all-to-all-start.1 = ((f32[32,2,16,8,128]{4,3,2,1,0:T(8,128)}), f32[32,2,16,8,128]{4,3,2,1,0:T(8,128)}, u32[]{:S(2)}, u32[]{:S(2)}) async-start(f32[32,2,16,8,128]{4,3,2,1,0:T(8,128)} %pack_green.1), calls=%async_computation.1 | async-start | bytes 8388608 | tf_op jit(solution)/shard_map/all_to_all | solution.py:421
  12.8 1.7 dynamic-slice_bitcast_fusion
  14.5 0.2 collective-permute-start
  14.7 0.6 pad_add_fusion.flags
  15.3 3.5 %collective-permute-done.other_ref = f32[2,1024,256]{2,1,0:T(8,128)} collective-permute-done((f32[2,1024,256]{2,1,0:T(8,128)S(1)}, f32[2,1024,256]{2,1,0:T(8,128)}, u32[]{:S(2)}, u32[]{:S(2)}) %collective-permute-start) | collective-permute-done | bytes 2097184 | tf_op jit(solution)/shard_map/ppermute | solution.py:420
  18.9 18.3 %form_sigma.1 = f32[32,2,16,8,128]{4,3,2,1,0:T(8,128)} custom-call(s32[2]{0:T(128)} %pad_add_fusion.flags, f32[2,2,1024,256]{3,2,1,0:T(8,128)} %bitcast.11, f32[2,1024,256]{2,1,0:T(8,128)} %collective-permute-done.other_ref, bf16[256,512]{1,0:T(8,128)(2,1)} %constant.48.clone.fh_ref, bf16[256,512]{1,0:T(8,128)(2,1)} %constant.49.clone.fl_ref, ...), custom_call_target="tpu_custom_call" | custom-call | flops 6442450944 | bytes 6291456 | tf_op jit(solution)/shard_map/form_sigma/pallas_call | solution.py:282
  37.2 101.1 %all-to-all-done.1 = f32[32,2,16,8,128]{4,3,2,1,0:T(8,128)} async-done(((f32[32,2,16,8,128]{4,3,2,1,0:T(8,128)}), f32[32,2,16,8,128]{4,3,2,1,0:T(8,128)}, u32[]{:S(2)}, u32[]{:S(2)}) %all-to-all-start.1) | async-done | bytes 4194336 | tf_op jit(solution)/shard_map/all_to_all | solution.py:421
  138.3 103.6 %all-to-all-start = ((f32[32,2,16,8,128]{4,3,2,1,0:T(8,128)}), f32[32,2,16,8,128]{4,3,2,1,0:T(8,128)}, u32[]{:S(2)}, u32[]{:S(2)}) async-start(f32[32,2,16,8,128]{4,3,2,1,0:T(8,128)} %form_sigma.1), calls=%async_computation | async-start | bytes 8388608 | tf_op jit(solution)/shard_map/all_to_all | solution.py:424
  241.9 13.7 %arrange_green.1.g_ref = bf16[8,2,2,256,256]{4,3,2,1,0:T(8,128)(2,1)} custom-call(f32[32,2,128,128]{3,2,1,0:T(8,128)} %bitcast.7.x_ref), custom_call_target="tpu_custom_call" | custom-call | bytes 8388608 | tf_op jit(solution)/shard_map/arrange_green/pallas_call | solution.py:335
  255.6 81.2 %all-to-all-done = f32[32,2,16,8,128]{4,3,2,1,0:T(8,128)} async-done(((f32[32,2,16,8,128]{4,3,2,1,0:T(8,128)}), f32[32,2,16,8,128]{4,3,2,1,0:T(8,128)}, u32[]{:S(2)}, u32[]{:S(2)}) %all-to-all-start) | async-done | bytes 4194336 | tf_op jit(solution)/shard_map/all_to_all | solution.py:424
  336.8 10.8 %collide.1 = f32[2,8,256,256]{3,2,1,0:T(8,128)} custom-call(f32[32,2,128,128]{3,2,1,0:T(8,128)} %bitcast.6.s_ref, bf16[8,2,2,256,256]{4,3,2,1,0:T(8,128)(2,1)} %arrange_green.1.g_ref), custom_call_target="tpu_custom_call" | custom-call | flops 3221225472 | bytes 12582912 | tf_op jit(solution)/shard_map/collide/pallas_call | solution.py:371
Async XLA Ops:
  5.3 133.0 %all-to-all-start.1 = ((f32[32,2,16,8,128]{4,3,2,1,0:T(8,128)}), f32[32,2,16,8,128]{4,3,2,1,0:T(8,128)}, u32[]{:S(2)}, u32[]{:S(2)}) async-start(f32[32,2,16,8,128]{4,3,2,1,0:T(8,128)} %pack_green.1), calls=%async_computation.1 | async-start | bytes 8388608 | tf_op jit(solution)/shard_map/all_to_all | solution.py:421
  14.5 4.3 %collective-permute-start = (f32[2,1024,256]{2,1,0:T(8,128)S(1)}, f32[2,1024,256]{2,1,0:T(8,128)}, u32[]{:S(2)}, u32[]{:S(2)}) collective-permute-start(f32[2,1024,256]{2,1,0:T(8,128)S(1)} %dynamic-slice_bitcast_fusion), channel_id=1, source_target_pairs={{0,1},{1,0},{2,8},{3,9},{4,16},{5,17},{6,24},{7,25},{8,3},{9,2},{1... | collective-permute-start | bytes 6291464 | tf_op jit(solution)/shard_map/ppermute | solution.py:420
  138.3 198.5 %all-to-all-start = ((f32[32,2,16,8,128]{4,3,2,1,0:T(8,128)}), f32[32,2,16,8,128]{4,3,2,1,0:T(8,128)}, u32[]{:S(2)}, u32[]{:S(2)}) async-start(f32[32,2,16,8,128]{4,3,2,1,0:T(8,128)} %form_sigma.1), calls=%async_computation | async-start | bytes 8388608 | tf_op jit(solution)/shard_map/all_to_all | solution.py:424

commit v2 on v1

--- a/solution.py
+++ b/solution.py
@@ -134,9 +134,13 @@
     return (z, 2 * a + c) if a < z else (z, 2 * a + 1 - c)
 
 
+def relay(a, b, rows_count):
+    return (a + rows_count // 2) % rows_count, b
+
+
 def block_plan(rows_count):
     cols_count = 2 * rows_count
-    route = []
+    route, first, second = [], [], []
     held = {}
     for a in range(rows_count):
         for b in range(cols_count):
@@ -144,10 +148,14 @@
             pa, pb = partner(a, b)
             target = pa * cols_count + pb
             keep = kept_half(a, b)
+            ra, rb = relay(a, b, rows_count)
+            middle = ra * cols_count + rb
             route.append((source, target))
+            first.append((source, middle))
+            second.append((middle, target))
             held[(2 * a + keep, b)] = (source, 0)
             held[(2 * a + 1 - keep, b)] = (target, 1)
-    return route, held
+    return route, first, second, held
 
 
 def split(x):
@@ -207,19 +215,19 @@
     )(x)
 
 
-def sigma_kernel(flags, kept_ref, other_ref, fh_ref, fl_ref, ih_ref, il_ref, out_ref, plus, minus):
+def sigma_kernel(flags, kept_ref, re_ref, im_ref, fh_ref, fl_ref, ih_ref, il_ref, out_ref, plus, minus):
     points, momenta = kept_ref.shape[2], kept_ref.shape[3]
     edge = math.isqrt(points)
     spans = points // LANES
     chunk = 256
     forward = (fh_ref[...], fl_ref[...])
 
-    for unit, ref in ((0, kept_ref.at[:, 0]), (1, other_ref)):
-
-        def transform(n, carry, unit=unit, ref=ref):
+    for unit, refs in enumerate(((kept_ref.at[0, 0], kept_ref.at[1, 0]), (re_ref, im_ref))):
+
+        def transform(n, carry, unit=unit, refs=refs):
             rows = pl.ds(pl.multiple_of(n * chunk, chunk), chunk)
-            y_re = dot3(split(ref[0, rows, :]), forward)
-            y_im = dot3(split(ref[1, rows, :]), forward)
+            y_re = dot3(split(refs[0][rows, :]), forward)
+            y_im = dot3(split(refs[1][rows, :]), forward)
             re_c, re_s = y_re[:, :momenta], y_re[:, momenta:]
             im_c, im_s = y_im[:, :momenta], y_im[:, momenta:]
             plus[unit, 0, rows, :] = re_c - im_s
@@ -273,8 +281,8 @@
         lax.fori_loop(0, spans // 2, combine, 0)
 
 
-def form_sigma(flags, x, other, tables):
-    comps, halves, points, momenta = x.shape
+def form_sigma(flags, x, other_re, other_im, tables):
+    comps, _, points, momenta = x.shape
     devices = momenta // SUBLANES
     spans = 2 * points // LANES
     whole = lambda a: pl.BlockSpec(a.shape, lambda n, s: (0,) * a.ndim)
@@ -286,7 +294,8 @@
             grid=(1,),
             in_specs=[
                 pl.BlockSpec((comps, 1, points, momenta), lambda n, s: (0, s[0], 0, 0)),
-                whole(other),
+                whole(other_re),
+                whole(other_im),
                 *[whole(t) for t in tables],
             ],
             out_specs=pl.BlockSpec(
@@ -299,11 +308,11 @@
         ),
         out_shape=jax.ShapeDtypeStruct((devices, comps, spans, SUBLANES, LANES), f32),
         cost_estimate=pl.CostEstimate(
-            flops=flops, bytes_accessed=3 * other.size * 4, transcendentals=0
+            flops=flops, bytes_accessed=6 * other_re.size * 4, transcendentals=0
         ),
         compiler_params=pltpu.CompilerParams(vmem_limit_bytes=56 * 1024 * 1024),
         name="form_sigma",
-    )(flags, x, other, *tables)
+    )(flags, x, other_re, other_im, *tables)
 
 
 def green_kernel(x_ref, out_ref, *, rows_count):
@@ -407,7 +416,7 @@
     comps, momenta, tile_rows, tile_cols = green_function.shape
     window = tile_rows * rows_count
     points = tile_cols * tile_cols
-    route, held = block_plan(rows_count)
+    route, first, second, held = block_plan(rows_count)
     a = lax.axis_index("tr")
     b = lax.axis_index("tc")
     z, c = b // 2, b % 2
@@ -416,21 +425,26 @@
 
     x = green_function.transpose(0, 2, 3, 1)
     halves = x.reshape(comps, 2, points, momenta)
-    leaving = lax.dynamic_index_in_dim(halves, 1 - keep, 1, keepdims=False)
-    other = lax.ppermute(leaving, axes, route)
-    green = lax.all_to_all(pack_green(x), axes, split_axis=0, concat_axis=0, tiled=True)
+    leaving = [
+        lax.dynamic_slice(halves, (n, 1 - keep, 0, 0), (1, 1, points, momenta)).reshape(
+            points, momenta
+        )
+        for n in range(comps)
+    ]
     tables = dft_tables(momenta)
-    sigma = form_sigma(jnp.stack([keep, diagonal]), halves, other, tables)
+    other_im = lax.ppermute(leaving[1], axes, first)
+    other_re = lax.ppermute(leaving[0], axes, route)
+    other_im = lax.ppermute(other_im, axes, second)
+    packed = pack_green(x)
+    green = lax.all_to_all(packed, axes, split_axis=0, concat_axis=0, tiled=True)
+    sigma = form_sigma(jnp.stack([keep, diagonal]), halves, other_re, other_im, tables)
     sigma = lax.all_to_all(sigma, axes, split_axis=0, concat_axis=0, tiled=True)
     green = arrange_green(green, rows_count, window)
     return collide(sigma, green, held, 2 * rows_count)
 
 
-def shards(green_function):
-    rows_count = lax.axis_size("tr")
-    cols_count = lax.axis_size("tc")
-    comps, momenta, tile_rows, tile_cols = green_function.shape
-    packs = (
+def is_packed(rows_count, cols_count, comps, momenta, tile_rows, tile_cols):
+    return (
         cols_count == 2 * rows_count
         and tile_rows == 2 * tile_cols
         and 4 * tile_cols == LANES
@@ -438,7 +452,11 @@
         and momenta % LANES == 0
         and cols_count % 4 == 0
     )
-    return packed_shards(green_function) if packs else general_shards(green_function)
+
+
+def shards(green_function):
+    sizes = (lax.axis_size("tr"), lax.axis_size("tc"), *green_function.shape)
+    return packed_shards(green_function) if is_packed(*sizes) else general_shards(green_function)
 
 
 def solution(mesh):

time: 348 us -> 289 us (0.83)
  starting transfers between devices: 111 us -> 61 us
  waiting for transfers between devices: 186 us -> 177 us
    all_to_all x1, waiting for transfers between devices: 101 us -> 8.85 us  [packed_shards(): lax.all_to_all(packed, axes, split_axis=0, concat_axis=0, tiled=True)]
    ppermute x1 -> x3, waiting for transfers between devices: 3.52 us -> 86.9 us  [the longest x1 59 us: packed_shards(): other_im = lax.ppermute(leaving[1], axes, first)]
    all_to_all x1, starting transfers between devices: 104 us -> 51.8 us  [packed_shards(): sigma = lax.all_to_all(sigma, axes, split_axis=0, concat_axis=0, tiled=True)]
  transfers between devices with their start and end apart: 3 -> 5, of which waited for: 3 -> 4; matrix products, arithmetic and copies ran while one was open for 1% -> 1% of each run, Pallas kernels for 9% -> 11%
where the time goes in v2:
time: 289 us
  waiting for transfers between devices  177 us (61%)
  starting transfers between devices  61 us (21%)
  Pallas kernels  48.2 us (17%)
    all_to_all x1, waiting for transfers between devices, packed_shards(): sigma = lax.all_to_all(sigma, axes, split_axis=0, concat_axis=0, tiled=True)  81.2 us
    ppermute x1, waiting for transfers between devices, packed_shards(): other_im = lax.ppermute(leaving[1], axes, first)  59 us
    all_to_all x1, starting transfers between devices, packed_shards(): sigma = lax.all_to_all(sigma, axes, split_axis=0, concat_axis=0, tiled=True)  51.8 us
    ppermute x1, waiting for transfers between devices, packed_shards(): other_im = lax.ppermute(other_im, axes, second)  27.9 us
    pallas_call x1, Pallas kernels, form_sigma(): pl.pallas_call(sigma_kernel, grid_spec=pltpu.PrefetchScalarGridSpec(num_s...  18.3 us
    pallas_call x1, Pallas kernels, arrange_green(): pl.pallas_call(functools.partial(green_kernel, rows_count=rows_count), gr...  13.7 us
    pallas_call x1, Pallas kernels, collide(): pl.pallas_call(functools.partial(collide_kernel, held=held, blocks=blocks...  10.8 us
    all_to_all x1, waiting for transfers between devices, packed_shards(): lax.all_to_all(packed, axes, split_axis=0, concat_axis=0, tiled=True)  8.85 us
  transfers between devices with their start and end apart: 5, of which 4 were waited for; matrix products, arithmetic and copies ran while one was open for 1% of the time, Pallas kernels for 11%

profile of v2, /device:TPU:0, one launch (start us, length us, event | category | flops | bytes accessed | tf_op | source)
XLA Modules:
  0.0 288.5 jit_solution(12729215521686927838)
XLA Ops:
  0.0 5.3 %pack_green.1 = f32[32,2,16,8,128]{4,3,2,1,0:T(8,128)} custom-call(f32[2,64,32,256]{3,2,1,0:T(8,128)} %bitcast.11), custom_call_target="tpu_custom_call" | custom-call | bytes 8388608 | tf_op jit(solution)/shard_map/pack_green/pallas_call | solution.py:205
  5.3 7.5 %all-to-all-start.1 = ((f32[32,2,16,8,128]{4,3,2,1,0:T(8,128)}), f32[32,2,16,8,128]{4,3,2,1,0:T(8,128)}, u32[]{:S(2)}, u32[]{:S(2)}) async-start(f32[32,2,16,8,128]{4,3,2,1,0:T(8,128)} %pack_green.1), calls=%async_computation.1 | async-start | bytes 8388608 | tf_op jit(solution)/shard_map/all_to_all | solution.py:439
  12.8 1.7 dynamic-slice_bitcast_fusion
  14.5 1.8 collective-permute-start.1
  16.2 0.0 collective-permute-start
  16.2 59.0 %collective-permute-done.1 = f32[1024,256]{1,0:T(8,128)S(1)} collective-permute-done((f32[1024,256]{1,0:T(8,128)S(1)}, f32[1024,256]{1,0:T(8,128)S(1)}, u32[]{:S(2)}, u32[]{:S(2)}) %collective-permute-start.1) | collective-permute-done | bytes 1048608 | tf_op jit(solution)/shard_map/ppermute | solution.py:435
  75.2 0.0 collective-permute-start.2
  75.2 0.6 pad_add_fusion.flags
  75.8 0.0 collective-permute-done.re_ref
  75.8 0.0 copy-start
  75.8 27.9 %collective-permute-done.2.im_ref = f32[1024,256]{1,0:T(8,128)} collective-permute-done((f32[1024,256]{1,0:T(8,128)S(1)}, f32[1024,256]{1,0:T(8,128)}, u32[]{:S(2)}, u32[]{:S(2)}) %collective-permute-start.2) | collective-permute-done | bytes 1048608 | tf_op jit(solution)/shard_map/ppermute | solution.py:437
  103.7 0.0 copy-done
  103.7 18.3 %form_sigma.1 = f32[32,2,16,8,128]{4,3,2,1,0:T(8,128)} custom-call(s32[2]{0:T(128)} %pad_add_fusion.flags, f32[2,2,1024,256]{3,2,1,0:T(8,128)} %bitcast.13, f32[1024,256]{1,0:T(8,128)} %copy-done, f32[1024,256]{1,0:T(8,128)} %collective-permute-done.2.im_ref, bf16[256,512]{1,0:T(8,128)(2,1)} %constant.44.clone.fh_ref, ...), custom_call_target="tpu_custom_call" | custom-call | flops 6442450944 | bytes 6291456 | tf_op jit(solution)/shard_map/form_sigma/pallas_call | solution.py:290
  122.1 8.8 %all-to-all-done.1 = f32[32,2,16,8,128]{4,3,2,1,0:T(8,128)} async-done(((f32[32,2,16,8,128]{4,3,2,1,0:T(8,128)}), f32[32,2,16,8,128]{4,3,2,1,0:T(8,128)}, u32[]{:S(2)}, u32[]{:S(2)}) %all-to-all-start.1) | async-done | bytes 4194336 | tf_op jit(solution)/shard_map/all_to_all | solution.py:439
  130.9 51.8 %all-to-all-start = ((f32[32,2,16,8,128]{4,3,2,1,0:T(8,128)}), f32[32,2,16,8,128]{4,3,2,1,0:T(8,128)}, u32[]{:S(2)}, u32[]{:S(2)}) async-start(f32[32,2,16,8,128]{4,3,2,1,0:T(8,128)} %form_sigma.1), calls=%async_computation | async-start | bytes 8388608 | tf_op jit(solution)/shard_map/all_to_all | solution.py:441
  182.8 13.7 %arrange_green.1.g_ref = bf16[8,2,2,256,256]{4,3,2,1,0:T(8,128)(2,1)} custom-call(f32[32,2,128,128]{3,2,1,0:T(8,128)} %bitcast.8.x_ref), custom_call_target="tpu_custom_call" | custom-call | bytes 8388608 | tf_op jit(solution)/shard_map/arrange_green/pallas_call | solution.py:344
  196.5 81.2 %all-to-all-done = f32[32,2,16,8,128]{4,3,2,1,0:T(8,128)} async-done(((f32[32,2,16,8,128]{4,3,2,1,0:T(8,128)}), f32[32,2,16,8,128]{4,3,2,1,0:T(8,128)}, u32[]{:S(2)}, u32[]{:S(2)}) %all-to-all-start) | async-done | bytes 4194336 | tf_op jit(solution)/shard_map/all_to_all | solution.py:441
  277.7 10.8 %collide.1 = f32[2,8,256,256]{3,2,1,0:T(8,128)} custom-call(f32[32,2,128,128]{3,2,1,0:T(8,128)} %bitcast.7.s_ref, bf16[8,2,2,256,256]{4,3,2,1,0:T(8,128)(2,1)} %arrange_green.1.g_ref), custom_call_target="tpu_custom_call" | custom-call | flops 3221225472 | bytes 12582912 | tf_op jit(solution)/shard_map/collide/pallas_call | solution.py:380
Async XLA Ops:
  5.3 125.6 %all-to-all-start.1 = ((f32[32,2,16,8,128]{4,3,2,1,0:T(8,128)}), f32[32,2,16,8,128]{4,3,2,1,0:T(8,128)}, u32[]{:S(2)}, u32[]{:S(2)}) async-start(f32[32,2,16,8,128]{4,3,2,1,0:T(8,128)} %pack_green.1), calls=%async_computation.1 | async-start | bytes 8388608 | tf_op jit(solution)/shard_map/all_to_all | solution.py:439
  14.5 60.7 %collective-permute-start.1 = (f32[1024,256]{1,0:T(8,128)S(1)}, f32[1024,256]{1,0:T(8,128)S(1)}, u32[]{:S(2)}, u32[]{:S(2)}) collective-permute-start(f32[1024,256]{1,0:T(8,128)S(1)} %get-tuple-element.5), channel_id=1, source_target_pairs={{0,16},{1,17},{2,18},{3,19},{4,20},{5,21},{6,22},{7,23},{8,24},{9,... | collective-permute-start | bytes 3145736 | tf_op jit(solution)/shard_map/ppermute | solution.py:435
  16.2 59.6 %collective-permute-start = (f32[1024,256]{1,0:T(8,128)S(1)}, f32[1024,256]{1,0:T(8,128)S(1)}, u32[]{:S(2)}, u32[]{:S(2)}) collective-permute-start(f32[1024,256]{1,0:T(8,128)S(1)} %get-tuple-element.6), channel_id=1, source_target_pairs={{0,1},{1,0},{2,8},{3,9},{4,16},{5,17},{6,24},{7,25},{8,3},{9,2},{1... | collective-permute-start | bytes 3145736 | tf_op jit(solution)/shard_map/ppermute | solution.py:436
  75.2 28.5 %collective-permute-start.2 = (f32[1024,256]{1,0:T(8,128)S(1)}, f32[1024,256]{1,0:T(8,128)}, u32[]{:S(2)}, u32[]{:S(2)}) collective-permute-start(f32[1024,256]{1,0:T(8,128)S(1)} %collective-permute-done.1), channel_id=1, source_target_pairs={{16,1},{17,0},{18,8},{19,9},{20,16},{21,17},{22,24},{23,25},{24,3}... | collective-permute-start | bytes 3145736 | tf_op jit(solution)/shard_map/ppermute | solution.py:437
  75.8 27.9 %copy-start = (f32[1024,256]{1,0:T(8,128)}, f32[1024,256]{1,0:T(8,128)S(1)}, u32[]{:S(2)}) copy-start(f32[1024,256]{1,0:T(8,128)S(1)} %collective-permute-done.re_ref) | copy-start | bytes 3145732
  130.9 146.8 %all-to-all-start = ((f32[32,2,16,8,128]{4,3,2,1,0:T(8,128)}), f32[32,2,16,8,128]{4,3,2,1,0:T(8,128)}, u32[]{:S(2)}, u32[]{:S(2)}) async-start(f32[32,2,16,8,128]{4,3,2,1,0:T(8,128)} %form_sigma.1), calls=%async_computation | async-start | bytes 8388608 | tf_op jit(solution)/shard_map/all_to_all | solution.py:441

commit v3 on v2

--- a/solution.py
+++ b/solution.py
@@ -191,26 +191,24 @@
 
 
 def send_kernel(x_ref, out_ref):
-    spans = out_ref.shape[2]
+    spans = out_ref.shape[1]
     for v in range(spans):
         rows = jnp.concatenate([x_ref[0, spans * q + v] for q in range(4)], 0)
-        out_ref[:, 0, v] = rows.T.reshape(out_ref.shape[0], SUBLANES, LANES)
-
-
-def pack_green(x):
-    comps, rows, cols, momenta = x.shape
+        out_ref[:, v] = rows.T.reshape(out_ref.shape[0], SUBLANES, LANES)
+
+
+def pack_green(x, comp):
+    _, rows, cols, momenta = x.shape
     spans = rows * cols // LANES
     devices = momenta // SUBLANES
     parts = momenta // LANES
     return pl.pallas_call(
         send_kernel,
-        grid=(comps, parts),
-        in_specs=[pl.BlockSpec((1, rows, cols, LANES), lambda c, p: (c, 0, 0, p))],
-        out_specs=pl.BlockSpec(
-            (devices // parts, 1, spans, SUBLANES, LANES), lambda c, p: (p, c, 0, 0, 0)
-        ),
-        out_shape=jax.ShapeDtypeStruct((devices, comps, spans, SUBLANES, LANES), f32),
-        cost_estimate=pl.CostEstimate(flops=0, bytes_accessed=2 * x.size * 4, transcendentals=0),
+        grid=(parts,),
+        in_specs=[pl.BlockSpec((1, rows, cols, LANES), lambda p: (comp, 0, 0, p))],
+        out_specs=pl.BlockSpec((devices // parts, spans, SUBLANES, LANES), lambda p: (p, 0, 0, 0)),
+        out_shape=jax.ShapeDtypeStruct((devices, spans, SUBLANES, LANES), f32),
+        cost_estimate=pl.CostEstimate(flops=0, bytes_accessed=x.size * 4, transcendentals=0),
         name="pack_green",
     )(x)
 
@@ -315,19 +313,19 @@
     )(flags, x, other_re, other_im, *tables)
 
 
-def green_kernel(x_ref, out_ref, *, rows_count):
+def green_kernel(re_ref, im_ref, out_ref, *, rows_count):
     cols_count = 2 * rows_count
     k = pl.program_id(0)
     tile_rows = out_ref.shape[3] // rows_count
     step = tile_rows // 4
-    for comp in range(2):
+    for comp, x_ref in enumerate((re_ref, im_ref)):
         for a in range(rows_count):
             for side in range(cols_count // 4):
                 groups = [[] for _ in range(4)]
                 for part in range(step // SUBLANES):
                     span = pl.ds(SUBLANES * SUBLANES * part + k, SUBLANES, stride=SUBLANES)
                     loaded = [
-                        x_ref[a * cols_count + 4 * side + n, comp, span, :] for n in range(4)
+                        x_ref[a * cols_count + 4 * side + n, span, :] for n in range(4)
                     ]
                     for q, value in enumerate(regroup(loaded)):
                         groups[q].append(value)
@@ -339,17 +337,19 @@
                     out_ref[0, comp, 1, rows, lanes] = low
 
 
-def arrange_green(x, rows_count, window):
-    x = x.reshape(x.shape[0], 2, -1, LANES)
+def arrange_green(parts, rows_count, window):
+    parts = [x.reshape(x.shape[0], -1, LANES) for x in parts]
     return pl.pallas_call(
         functools.partial(green_kernel, rows_count=rows_count),
         grid=(SUBLANES,),
-        in_specs=[pl.BlockSpec(x.shape, lambda k: (0, 0, 0, 0))],
+        in_specs=[pl.BlockSpec(x.shape, lambda k: (0, 0, 0)) for x in parts],
         out_specs=pl.BlockSpec((1, 2, 2, window, window), lambda k: (k, 0, 0, 0, 0)),
         out_shape=jax.ShapeDtypeStruct((SUBLANES, 2, 2, window, window), bf16),
-        cost_estimate=pl.CostEstimate(flops=0, bytes_accessed=2 * x.size * 4, transcendentals=0),
+        cost_estimate=pl.CostEstimate(
+            flops=0, bytes_accessed=4 * parts[0].size * 4, transcendentals=0
+        ),
         name="arrange_green",
-    )(x)
+    )(*parts)
 
 
 def collide_kernel(s_ref, g_ref, out_ref, left, *, held, blocks):
@@ -435,8 +435,9 @@
     other_im = lax.ppermute(leaving[1], axes, first)
     other_re = lax.ppermute(leaving[0], axes, route)
     other_im = lax.ppermute(other_im, axes, second)
-    packed = pack_green(x)
-    green = lax.all_to_all(packed, axes, split_axis=0, concat_axis=0, tiled=True)
+    green = [pack_green(x, comp) for comp in range(comps)]
+    for comp in range(comps):
+        green[comp] = lax.all_to_all(green[comp], axes, split_axis=0, concat_axis=0, tiled=True)
     sigma = form_sigma(jnp.stack([keep, diagonal]), halves, other_re, other_im, tables)
     sigma = lax.all_to_all(sigma, axes, split_axis=0, concat_axis=0, tiled=True)
     green = arrange_green(green, rows_count, window)

time: 289 us -> 331 us (1.15)
  starting transfers between devices: 61 us -> 86.4 us
  waiting for transfers between devices: 177 us -> 193 us
    all_to_all x1 -> x2, waiting for transfers between devices: 8.85 us -> 47.1 us  [packed_shards(): lax.all_to_all(green[comp], axes, split_axis=0, concat_axis=0, tiled=True)]
    ppermute x1, starting transfers between devices: 0.01 us -> 26.2 us  [packed_shards(): other_im = lax.ppermute(other_im, axes, second)]
    ppermute x1, waiting for transfers between devices: 59 us -> 42.1 us  [packed_shards(): other_im = lax.ppermute(leaving[1], axes, first)]
    ppermute x1, waiting for transfers between devices: 27.9 us -> 22.7 us  [packed_shards(): other_im = lax.ppermute(other_im, axes, second)]
    all_to_all x1, starting transfers between devices: 51.8 us -> 47.7 us  [packed_shards(): sigma = lax.all_to_all(sigma, axes, split_axis=0, concat_axis=0, tiled=True)]
    all_to_all x1 -> x2, starting transfers between devices: 7.45 us -> 10.9 us  [packed_shards(): lax.all_to_all(green[comp], axes, split_axis=0, concat_axis=0, tiled=True)]
  transfers between devices with their start and end apart: 5 -> 6, of which waited for: 4 -> 4; matrix products, arithmetic and copies ran while one was open for 1% -> 1% of each run, Pallas kernels for 11% -> 11%
where the time goes in v3:
time: 331 us
  waiting for transfers between devices  193 us (58%)
  starting transfers between devices  86.4 us (26%)
  Pallas kernels  48.8 us (15%)
    all_to_all x1, waiting for transfers between devices, packed_shards(): sigma = lax.all_to_all(sigma, axes, split_axis=0, concat_axis=0, tiled=True)  81.1 us
    all_to_all x1, starting transfers between devices, packed_shards(): sigma = lax.all_to_all(sigma, axes, split_axis=0, concat_axis=0, tiled=True)  47.7 us
    all_to_all x2, waiting for transfers between devices, packed_shards(): lax.all_to_all(green[comp], axes, split_axis=0, concat_axis=0, tiled=True)  47.1 us
    ppermute x1, waiting for transfers between devices, packed_shards(): other_im = lax.ppermute(leaving[1], axes, first)  42.1 us
    ppermute x1, starting transfers between devices, packed_shards(): other_im = lax.ppermute(other_im, axes, second)  26.2 us
    ppermute x1, waiting for transfers between devices, packed_shards(): other_im = lax.ppermute(other_im, axes, second)  22.7 us
    pallas_call x1, Pallas kernels, form_sigma(): pl.pallas_call(sigma_kernel, grid_spec=pltpu.PrefetchScalarGridSpec(num_s...  18.3 us
    pallas_call x1, Pallas kernels, arrange_green(): pl.pallas_call(functools.partial(green_kernel, rows_count=rows_count), gr...  13.8 us
  transfers between devices with their start and end apart: 6, of which 4 were waited for; matrix products, arithmetic and copies ran while one was open for 1% of the time, Pallas kernels for 11%

profile of v3, /device:TPU:0, one launch (start us, length us, event | category | flops | bytes accessed | tf_op | source)
XLA Modules:
  0.0 330.6 jit_solution(17331834740874715074)
XLA Ops:
  0.0 2.9 pack_green.2
  2.9 7.3 %all-to-all-start.1 = ((f32[32,16,8,128]{3,2,1,0:T(8,128)}), f32[32,16,8,128]{3,2,1,0:T(8,128)S(1)}, u32[]{:S(2)}, u32[]{:S(2)}) async-start(f32[32,16,8,128]{3,2,1,0:T(8,128)} %pack_green.2), calls=%async_computation.1 | async-start | bytes 4194304 | tf_op jit(solution)/shard_map/all_to_all | solution.py:440
  10.2 2.9 pack_green.3
  13.1 47.1 %all-to-all-done.1 = f32[32,16,8,128]{3,2,1,0:T(8,128)S(1)} async-done(((f32[32,16,8,128]{3,2,1,0:T(8,128)}), f32[32,16,8,128]{3,2,1,0:T(8,128)S(1)}, u32[]{:S(2)}, u32[]{:S(2)}) %all-to-all-start.1) | async-done | bytes 2097184 | tf_op jit(solution)/shard_map/all_to_all | solution.py:440
  60.2 0.0 copy-start
  60.2 3.6 %all-to-all-start.2 = ((f32[32,16,8,128]{3,2,1,0:T(8,128)}), f32[32,16,8,128]{3,2,1,0:T(8,128)}, u32[]{:S(2)}, u32[]{:S(2)}) async-start(f32[32,16,8,128]{3,2,1,0:T(8,128)} %pack_green.3), calls=%async_computation.2 | async-start | bytes 4194304 | tf_op jit(solution)/shard_map/all_to_all | solution.py:440
  63.9 1.7 dynamic-slice_bitcast_fusion
  65.5 0.0 copy-done
  65.5 1.6 collective-permute-start.1
  67.2 0.0 collective-permute-start
  67.2 42.1 %collective-permute-done.1 = f32[1024,256]{1,0:T(8,128)S(1)} collective-permute-done((f32[1024,256]{1,0:T(8,128)S(1)}, f32[1024,256]{1,0:T(8,128)S(1)}, u32[]{:S(2)}, u32[]{:S(2)}) %collective-permute-start.1) | collective-permute-done | bytes 1048608 | tf_op jit(solution)/shard_map/ppermute | solution.py:435
  109.3 26.2 %collective-permute-start.2 = (f32[1024,256]{1,0:T(8,128)S(1)}, f32[1024,256]{1,0:T(8,128)}, u32[]{:S(2)}, u32[]{:S(2)}) collective-permute-start(f32[1024,256]{1,0:T(8,128)S(1)} %collective-permute-done.1), channel_id=1, source_target_pairs={{16,1},{17,0},{18,8},{19,9},{20,16},{21,17},{22,24},{23,25},{24,3}... | collective-permute-start | bytes 3145736 | tf_op jit(solution)/shard_map/ppermute | solution.py:437
  135.5 0.6 pad_add_fusion.flags
  136.1 0.0 collective-permute-done.re_ref
  136.1 0.0 copy-start.1
  136.1 22.7 %collective-permute-done.2.im_ref = f32[1024,256]{1,0:T(8,128)} collective-permute-done((f32[1024,256]{1,0:T(8,128)S(1)}, f32[1024,256]{1,0:T(8,128)}, u32[]{:S(2)}, u32[]{:S(2)}) %collective-permute-start.2) | collective-permute-done | bytes 1048608 | tf_op jit(solution)/shard_map/ppermute | solution.py:437
  158.8 0.0 copy-done.1
  158.8 18.3 %form_sigma.1 = f32[32,2,16,8,128]{4,3,2,1,0:T(8,128)} custom-call(s32[2]{0:T(128)} %pad_add_fusion.flags, f32[2,2,1024,256]{3,2,1,0:T(8,128)} %bitcast.15, f32[1024,256]{1,0:T(8,128)} %copy-done.1, f32[1024,256]{1,0:T(8,128)} %collective-permute-done.2.im_ref, bf16[256,512]{1,0:T(8,128)(2,1)} %constant.44.clone.fh_ref, ...), custom_call_target="tpu_custom_call" | custom-call | flops 6442450944 | bytes 6291456 | tf_op jit(solution)/shard_map/form_sigma/pallas_call | solution.py:288
  177.1 0.0 all-to-all-done.2
  177.1 47.7 %all-to-all-start = ((f32[32,2,16,8,128]{4,3,2,1,0:T(8,128)}), f32[32,2,16,8,128]{4,3,2,1,0:T(8,128)}, u32[]{:S(2)}, u32[]{:S(2)}) async-start(f32[32,2,16,8,128]{4,3,2,1,0:T(8,128)} %form_sigma.1), calls=%async_computation | async-start | bytes 8388608 | tf_op jit(solution)/shard_map/all_to_all | solution.py:442
  224.8 13.8 %arrange_green.1.g_ref = bf16[8,2,2,256,256]{4,3,2,1,0:T(8,128)(2,1)} custom-call(f32[32,128,128]{2,1,0:T(8,128)} %bitcast.16, f32[32,128,128]{2,1,0:T(8,128)} %bitcast.9.im_ref), custom_call_target="tpu_custom_call" | custom-call | bytes 8388608 | tf_op jit(solution)/shard_map/arrange_green/pallas_call | solution.py:342
  238.7 81.1 %all-to-all-done = f32[32,2,16,8,128]{4,3,2,1,0:T(8,128)} async-done(((f32[32,2,16,8,128]{4,3,2,1,0:T(8,128)}), f32[32,2,16,8,128]{4,3,2,1,0:T(8,128)}, u32[]{:S(2)}, u32[]{:S(2)}) %all-to-all-start) | async-done | bytes 4194336 | tf_op jit(solution)/shard_map/all_to_all | solution.py:442
  319.8 10.8 %collide.1 = f32[2,8,256,256]{3,2,1,0:T(8,128)} custom-call(f32[32,2,128,128]{3,2,1,0:T(8,128)} %bitcast.7.s_ref, bf16[8,2,2,256,256]{4,3,2,1,0:T(8,128)(2,1)} %arrange_green.1.g_ref), custom_call_target="tpu_custom_call" | custom-call | flops 3221225472 | bytes 12582912 | tf_op jit(solution)/shard_map/collide/pallas_call | solution.py:380
Async XLA Ops:
  2.9 57.4 %all-to-all-start.1 = ((f32[32,16,8,128]{3,2,1,0:T(8,128)}), f32[32,16,8,128]{3,2,1,0:T(8,128)S(1)}, u32[]{:S(2)}, u32[]{:S(2)}) async-start(f32[32,16,8,128]{3,2,1,0:T(8,128)} %pack_green.2), calls=%async_computation.1 | async-start | bytes 4194304 | tf_op jit(solution)/shard_map/all_to_all | solution.py:440
  60.2 5.3 %copy-start = (f32[32,16,8,128]{3,2,1,0:T(8,128)}, f32[32,16,8,128]{3,2,1,0:T(8,128)S(1)}, u32[]{:S(2)}) copy-start(f32[32,16,8,128]{3,2,1,0:T(8,128)S(1)} %all-to-all-done.1) | copy-start | bytes 6291460
  60.2 116.9 %all-to-all-start.2 = ((f32[32,16,8,128]{3,2,1,0:T(8,128)}), f32[32,16,8,128]{3,2,1,0:T(8,128)}, u32[]{:S(2)}, u32[]{:S(2)}) async-start(f32[32,16,8,128]{3,2,1,0:T(8,128)} %pack_green.3), calls=%async_computation.2 | async-start | bytes 4194304 | tf_op jit(solution)/shard_map/all_to_all | solution.py:440
  65.5 43.7 %collective-permute-start.1 = (f32[1024,256]{1,0:T(8,128)S(1)}, f32[1024,256]{1,0:T(8,128)S(1)}, u32[]{:S(2)}, u32[]{:S(2)}) collective-permute-start(f32[1024,256]{1,0:T(8,128)S(1)} %get-tuple-element.5), channel_id=1, source_target_pairs={{0,16},{1,17},{2,18},{3,19},{4,20},{5,21},{6,22},{7,23},{8,24},{9,... | collective-permute-start | bytes 3145736 | tf_op jit(solution)/shard_map/ppermute | solution.py:435
  67.2 68.9 %collective-permute-start = (f32[1024,256]{1,0:T(8,128)S(1)}, f32[1024,256]{1,0:T(8,128)S(1)}, u32[]{:S(2)}, u32[]{:S(2)}) collective-permute-start(f32[1024,256]{1,0:T(8,128)S(1)} %get-tuple-element.6), channel_id=1, source_target_pairs={{0,1},{1,0},{2,8},{3,9},{4,16},{5,17},{6,24},{7,25},{8,3},{9,2},{1... | collective-permute-start | bytes 3145736 | tf_op jit(solution)/shard_map/ppermute | solution.py:436
  109.3 49.5 %collective-permute-start.2 = (f32[1024,256]{1,0:T(8,128)S(1)}, f32[1024,256]{1,0:T(8,128)}, u32[]{:S(2)}, u32[]{:S(2)}) collective-permute-start(f32[1024,256]{1,0:T(8,128)S(1)} %collective-permute-done.1), channel_id=1, source_target_pairs={{16,1},{17,0},{18,8},{19,9},{20,16},{21,17},{22,24},{23,25},{24,3}... | collective-permute-start | bytes 3145736 | tf_op jit(solution)/shard_map/ppermute | solution.py:437
  136.1 22.7 %copy-start.1 = (f32[1024,256]{1,0:T(8,128)}, f32[1024,256]{1,0:T(8,128)S(1)}, u32[]{:S(2)}) copy-start(f32[1024,256]{1,0:T(8,128)S(1)} %collective-permute-done.re_ref) | copy-start | bytes 3145732
  177.1 142.6 %all-to-all-start = ((f32[32,2,16,8,128]{4,3,2,1,0:T(8,128)}), f32[32,2,16,8,128]{4,3,2,1,0:T(8,128)}, u32[]{:S(2)}, u32[]{:S(2)}) async-start(f32[32,2,16,8,128]{4,3,2,1,0:T(8,128)} %form_sigma.1), calls=%async_computation | async-start | bytes 8388608 | tf_op jit(solution)/shard_map/all_to_all | solution.py:442

commit v4 on v3

--- a/solution.py
+++ b/solution.py
@@ -134,28 +134,28 @@
     return (z, 2 * a + c) if a < z else (z, 2 * a + 1 - c)
 
 
-def relay(a, b, rows_count):
-    return (a + rows_count // 2) % rows_count, b
+def ways(rows_count):
+    return (0, 1, rows_count // 2, rows_count // 2 + 1)
 
 
 def block_plan(rows_count):
     cols_count = 2 * rows_count
-    route, first, second = [], [], []
+    first = [[] for _ in ways(rows_count)]
+    second = [[] for _ in ways(rows_count)]
     held = {}
     for a in range(rows_count):
         for b in range(cols_count):
             source = a * cols_count + b
             pa, pb = partner(a, b)
             target = pa * cols_count + pb
+            for n, flip in enumerate(ways(rows_count)):
+                middle = (a ^ flip) * cols_count + b
+                first[n].append((source, middle))
+                second[n].append((middle, target))
             keep = kept_half(a, b)
-            ra, rb = relay(a, b, rows_count)
-            middle = ra * cols_count + rb
-            route.append((source, target))
-            first.append((source, middle))
-            second.append((middle, target))
             held[(2 * a + keep, b)] = (source, 0)
             held[(2 * a + 1 - keep, b)] = (target, 1)
-    return route, first, second, held
+    return first, second, held
 
 
 def split(x):
@@ -213,19 +213,26 @@
     )(x)
 
 
-def sigma_kernel(flags, kept_ref, re_ref, im_ref, fh_ref, fl_ref, ih_ref, il_ref, out_ref, plus, minus):
+def sigma_kernel(flags, kept_ref, re0_ref, re1_ref, im0_ref, im1_ref, fh_ref, fl_ref, ih_ref, il_ref, out_ref, plus, minus):
     points, momenta = kept_ref.shape[2], kept_ref.shape[3]
     edge = math.isqrt(points)
     spans = points // LANES
     chunk = 256
     forward = (fh_ref[...], fl_ref[...])
 
-    for unit, refs in enumerate(((kept_ref.at[0, 0], kept_ref.at[1, 0]), (re_ref, im_ref))):
-
-        def transform(n, carry, unit=unit, refs=refs):
-            rows = pl.ds(pl.multiple_of(n * chunk, chunk), chunk)
-            y_re = dot3(split(refs[0][rows, :]), forward)
-            y_im = dot3(split(refs[1][rows, :]), forward)
+    half = points // 2
+    pieces = (
+        (0, 0, points, kept_ref.at[0, 0], kept_ref.at[1, 0]),
+        (1, 0, half, re0_ref, im0_ref),
+        (1, half, half, re1_ref, im1_ref),
+    )
+    for unit, start, count, re_ref, im_ref in pieces:
+
+        def transform(n, carry, unit=unit, start=start, re_ref=re_ref, im_ref=im_ref):
+            source = pl.ds(pl.multiple_of(n * chunk, chunk), chunk)
+            rows = pl.ds(pl.multiple_of(start + n * chunk, chunk), chunk)
+            y_re = dot3(split(re_ref[source, :]), forward)
+            y_im = dot3(split(im_ref[source, :]), forward)
             re_c, re_s = y_re[:, :momenta], y_re[:, momenta:]
             im_c, im_s = y_im[:, :momenta], y_im[:, momenta:]
             plus[unit, 0, rows, :] = re_c - im_s
@@ -238,7 +245,7 @@
                 minus[unit, 1, p, rows, :] = m_im[:, lanes]
             return carry
 
-        lax.fori_loop(0, points // chunk, transform, 0)
+        lax.fori_loop(0, count // chunk, transform, 0)
 
     inverse = (ih_ref[...], il_ref[...])
     diagonal = flags[1]
@@ -279,7 +286,7 @@
         lax.fori_loop(0, spans // 2, combine, 0)
 
 
-def form_sigma(flags, x, other_re, other_im, tables):
+def form_sigma(flags, x, others, tables):
     comps, _, points, momenta = x.shape
     devices = momenta // SUBLANES
     spans = 2 * points // LANES
@@ -292,8 +299,7 @@
             grid=(1,),
             in_specs=[
                 pl.BlockSpec((comps, 1, points, momenta), lambda n, s: (0, s[0], 0, 0)),
-                whole(other_re),
-                whole(other_im),
+                *[whole(t) for t in others],
                 *[whole(t) for t in tables],
             ],
             out_specs=pl.BlockSpec(
@@ -306,11 +312,11 @@
         ),
         out_shape=jax.ShapeDtypeStruct((devices, comps, spans, SUBLANES, LANES), f32),
         cost_estimate=pl.CostEstimate(
-            flops=flops, bytes_accessed=6 * other_re.size * 4, transcendentals=0
+            flops=flops, bytes_accessed=12 * others[0].size * 4, transcendentals=0
         ),
         compiler_params=pltpu.CompilerParams(vmem_limit_bytes=56 * 1024 * 1024),
         name="form_sigma",
-    )(flags, x, other_re, other_im, *tables)
+    )(flags, x, *others, *tables)
 
 
 def green_kernel(re_ref, im_ref, out_ref, *, rows_count):
@@ -416,7 +422,7 @@
     comps, momenta, tile_rows, tile_cols = green_function.shape
     window = tile_rows * rows_count
     points = tile_cols * tile_cols
-    route, first, second, held = block_plan(rows_count)
+    first, second, held = block_plan(rows_count)
     a = lax.axis_index("tr")
     b = lax.axis_index("tc")
     z, c = b // 2, b % 2
@@ -425,20 +431,23 @@
 
     x = green_function.transpose(0, 2, 3, 1)
     halves = x.reshape(comps, 2, points, momenta)
+    half = points // 2
     leaving = [
-        lax.dynamic_slice(halves, (n, 1 - keep, 0, 0), (1, 1, points, momenta)).reshape(
-            points, momenta
-        )
-        for n in range(comps)
+        lax.dynamic_slice(
+            halves, (n // 2, 1 - keep, half * (n % 2), 0), (1, 1, half, momenta)
+        ).reshape(half, momenta)
+        for n in range(4)
     ]
     tables = dft_tables(momenta)
-    other_im = lax.ppermute(leaving[1], axes, first)
-    other_re = lax.ppermute(leaving[0], axes, route)
-    other_im = lax.ppermute(other_im, axes, second)
+    others = list(leaving)
+    for n in range(1, 4):
+        others[n] = lax.ppermute(others[n], axes, first[n])
+    for n in range(4):
+        others[n] = lax.ppermute(others[n], axes, second[n])
     green = [pack_green(x, comp) for comp in range(comps)]
     for comp in range(comps):
         green[comp] = lax.all_to_all(green[comp], axes, split_axis=0, concat_axis=0, tiled=True)
-    sigma = form_sigma(jnp.stack([keep, diagonal]), halves, other_re, other_im, tables)
+    sigma = form_sigma(jnp.stack([keep, diagonal]), halves, others, tables)
     sigma = lax.all_to_all(sigma, axes, split_axis=0, concat_axis=0, tiled=True)
     green = arrange_green(green, rows_count, window)
     return collide(sigma, green, held, 2 * rows_count)
@@ -452,6 +461,7 @@
         and momenta == SUBLANES * rows_count * cols_count
         and momenta % LANES == 0
         and cols_count % 4 == 0
+        and rows_count & (rows_count - 1) == 0
     )
 
 

time: 331 us -> 291 us (0.88)
  starting transfers between devices: 86.4 us -> 31 us
  waiting for transfers between devices: 193 us -> 209 us
    all_to_all x1, starting transfers between devices: 47.7 us -> 5.9 us  [packed_shards(): sigma = lax.all_to_all(sigma, axes, split_axis=0, concat_axis=0, tiled=True)]
    ppermute x3 -> x7, waiting for transfers between devices: 64.8 us -> 80.4 us  [the longest x3 52.2 us: packed_shards(): others[n] = lax.ppermute(others[n], axes, first[n])]
    ppermute x3 -> x7, starting transfers between devices: 27.9 us -> 14.2 us  [the longest x4 10.7 us: packed_shards(): others[n] = lax.ppermute(others[n], axes, second[n])]
  transfers between devices with their start and end apart: 6 -> 10, of which waited for: 4 -> 7; matrix products, arithmetic and copies ran while one was open for 1% -> 1% of each run, Pallas kernels for 11% -> 12%
where the time goes in v4:
time: 291 us
  waiting for transfers between devices  209 us (72%)
  Pallas kernels  48.8 us (17%)
  starting transfers between devices  31 us (11%)
    all_to_all x1, waiting for transfers between devices, packed_shards(): sigma = lax.all_to_all(sigma, axes, split_axis=0, concat_axis=0, tiled=True)  81.1 us
    ppermute x3, waiting for transfers between devices, packed_shards(): others[n] = lax.ppermute(others[n], axes, first[n])  52.2 us
    all_to_all x2, waiting for transfers between devices, packed_shards(): lax.all_to_all(green[comp], axes, split_axis=0, concat_axis=0, tiled=True)  47.1 us
    ppermute x4, waiting for transfers between devices, packed_shards(): others[n] = lax.ppermute(others[n], axes, second[n])  28.2 us
    pallas_call x1, Pallas kernels, form_sigma(): pl.pallas_call(sigma_kernel, grid_spec=pltpu.PrefetchScalarGridSpec(num_s...  18.3 us
    pallas_call x1, Pallas kernels, arrange_green(): pl.pallas_call(functools.partial(green_kernel, rows_count=rows_count), gr...  13.8 us
    all_to_all x2, starting transfers between devices, packed_shards(): lax.all_to_all(green[comp], axes, split_axis=0, concat_axis=0, tiled=True)  10.9 us
    pallas_call x1, Pallas kernels, collide(): pl.pallas_call(functools.partial(collide_kernel, held=held, blocks=blocks...  10.8 us
  transfers between devices with their start and end apart: 10, of which 7 were waited for; matrix products, arithmetic and copies ran while one was open for 1% of the time, Pallas kernels for 12%

profile of v4, /device:TPU:0, one launch (start us, length us, event | category | flops | bytes accessed | tf_op | source)
XLA Modules:
  0.0 290.9 jit_solution(165706086226529763)
XLA Ops:
  0.0 2.9 pack_green.2
  2.9 7.3 %all-to-all-start.1 = ((f32[32,16,8,128]{3,2,1,0:T(8,128)}), f32[32,16,8,128]{3,2,1,0:T(8,128)S(1)}, u32[]{:S(2)}, u32[]{:S(2)}) async-start(f32[32,16,8,128]{3,2,1,0:T(8,128)} %pack_green.2), calls=%async_computation.1 | async-start | bytes 4194304 | tf_op jit(solution)/shard_map/all_to_all | solution.py:449
  10.2 2.9 %pack_green.3 = f32[32,16,8,128]{3,2,1,0:T(8,128)} custom-call(f32[2,64,32,256]{3,2,1,0:T(8,128)} %bitcast.17), custom_call_target="tpu_custom_call" | custom-call | bytes 4194304 | tf_op jit(solution)/shard_map/pack_green/pallas_call | solution.py:205
  13.1 47.1 %all-to-all-done.1 = f32[32,16,8,128]{3,2,1,0:T(8,128)S(1)} async-done(((f32[32,16,8,128]{3,2,1,0:T(8,128)}), f32[32,16,8,128]{3,2,1,0:T(8,128)S(1)}, u32[]{:S(2)}, u32[]{:S(2)}) %all-to-all-start.1) | async-done | bytes 2097184 | tf_op jit(solution)/shard_map/all_to_all | solution.py:449
  60.2 0.0 copy-start
  60.2 3.6 %all-to-all-start.2 = ((f32[32,16,8,128]{3,2,1,0:T(8,128)}), f32[32,16,8,128]{3,2,1,0:T(8,128)}, u32[]{:S(2)}, u32[]{:S(2)}) async-start(f32[32,16,8,128]{3,2,1,0:T(8,128)} %pack_green.3), calls=%async_computation.2 | async-start | bytes 4194304 | tf_op jit(solution)/shard_map/all_to_all | solution.py:449
  63.9 1.7 dynamic-slice_bitcast_fusion
  65.5 0.0 copy-done
  65.5 2.6 collective-permute-start.5
  68.1 0.5 collective-permute-start.3
  68.6 0.5 collective-permute-start.1
  69.1 0.0 collective-permute-start
  69.1 46.3 %collective-permute-done.5 = f32[512,256]{1,0:T(8,128)S(1)} collective-permute-done((f32[512,256]{1,0:T(8,128)S(1)}, f32[512,256]{1,0:T(8,128)S(1)}, u32[]{:S(2)}, u32[]{:S(2)}) %collective-permute-start.5) | collective-permute-done | bytes 524320 | tf_op jit(solution)/shard_map/ppermute | solution.py:444
  115.4 10.7 %collective-permute-start.6 = (f32[512,256]{1,0:T(8,128)S(1)}, f32[512,256]{1,0:T(8,128)S(1)}, u32[]{:S(2)}, u32[]{:S(2)}) collective-permute-start(f32[512,256]{1,0:T(8,128)S(1)} %collective-permute-done.5), channel_id=1, source_target_pairs={{24,1},{25,0},{26,8},{27,9},{28,16},{29,17},{30,24},{31,25},{16,3}... | collective-permute-start | bytes 1572872 | tf_op jit(solution)/shard_map/ppermute | solution.py:446
  126.1 0.0 collective-permute-done.3
  126.1 0.0 collective-permute-start.4
  126.1 5.9 %collective-permute-done.1 = f32[512,256]{1,0:T(8,128)S(1)} collective-permute-done((f32[512,256]{1,0:T(8,128)S(1)}, f32[512,256]{1,0:T(8,128)S(1)}, u32[]{:S(2)}, u32[]{:S(2)}) %collective-permute-start.1) | collective-permute-done | bytes 524320 | tf_op jit(solution)/shard_map/ppermute | solution.py:444
  132.0 0.0 collective-permute-start.2
  132.0 0.7 pad_add_fusion.flags
  132.7 0.0 collective-permute-done.re0_ref
  132.7 0.0 copy-start.1
  132.7 5.8 %collective-permute-done.6.im1_ref = f32[512,256]{1,0:T(8,128)S(1)} collective-permute-done((f32[512,256]{1,0:T(8,128)S(1)}, f32[512,256]{1,0:T(8,128)S(1)}, u32[]{:S(2)}, u32[]{:S(2)}) %collective-permute-start.6) | collective-permute-done | bytes 524320 | tf_op jit(solution)/shard_map/ppermute | solution.py:446
  138.4 11.2 %collective-permute-done.4.im0_ref = f32[512,256]{1,0:T(8,128)} collective-permute-done((f32[512,256]{1,0:T(8,128)S(1)}, f32[512,256]{1,0:T(8,128)}, u32[]{:S(2)}, u32[]{:S(2)}) %collective-permute-start.4) | collective-permute-done | bytes 524320 | tf_op jit(solution)/shard_map/ppermute | solution.py:446
  149.7 11.2 %collective-permute-done.2.re1_ref = f32[512,256]{1,0:T(8,128)} collective-permute-done((f32[512,256]{1,0:T(8,128)S(1)}, f32[512,256]{1,0:T(8,128)}, u32[]{:S(2)}, u32[]{:S(2)}) %collective-permute-start.2) | collective-permute-done | bytes 524320 | tf_op jit(solution)/shard_map/ppermute | solution.py:446
  160.8 0.0 copy-done.1
  160.8 0.0 copy-done.2
  160.8 18.3 %form_sigma.1 = f32[32,2,16,8,128]{4,3,2,1,0:T(8,128)} custom-call(s32[2]{0:T(128)} %pad_add_fusion.flags, f32[2,2,1024,256]{3,2,1,0:T(8,128)} %bitcast.19, f32[512,256]{1,0:T(8,128)} %copy-done.1, f32[512,256]{1,0:T(8,128)} %collective-permute-done.2.re1_ref, f32[512,256]{1,0:T(8,128)} %collective-permute-done.4.im0_ref, f32[512,256]{1,0:T(8,128)} %copy-done.2, ...), custom_call_target="tpu_custom_call" | custom-call | flops 6442450944 | bytes 6291456 | tf_op jit(solution)/shard_map/form_sigma/pallas_call | solution.py:295
  179.2 0.0 all-to-all-done.2
  179.2 5.9 %all-to-all-start = ((f32[32,2,16,8,128]{4,3,2,1,0:T(8,128)}), f32[32,2,16,8,128]{4,3,2,1,0:T(8,128)}, u32[]{:S(2)}, u32[]{:S(2)}) async-start(f32[32,2,16,8,128]{4,3,2,1,0:T(8,128)} %form_sigma.1), calls=%async_computation | async-start | bytes 8388608 | tf_op jit(solution)/shard_map/all_to_all | solution.py:451
  185.1 13.8 %arrange_green.1.g_ref = bf16[8,2,2,256,256]{4,3,2,1,0:T(8,128)(2,1)} custom-call(f32[32,128,128]{2,1,0:T(8,128)} %bitcast.20, f32[32,128,128]{2,1,0:T(8,128)} %bitcast.11.im_ref), custom_call_target="tpu_custom_call" | custom-call | bytes 8388608 | tf_op jit(solution)/shard_map/arrange_green/pallas_call | solution.py:348
  198.9 81.1 %all-to-all-done = f32[32,2,16,8,128]{4,3,2,1,0:T(8,128)} async-done(((f32[32,2,16,8,128]{4,3,2,1,0:T(8,128)}), f32[32,2,16,8,128]{4,3,2,1,0:T(8,128)}, u32[]{:S(2)}, u32[]{:S(2)}) %all-to-all-start) | async-done | bytes 4194336 | tf_op jit(solution)/shard_map/all_to_all | solution.py:451
  280.0 10.8 %collide.1 = f32[2,8,256,256]{3,2,1,0:T(8,128)} custom-call(f32[32,2,128,128]{3,2,1,0:T(8,128)} %bitcast.9.s_ref, bf16[8,2,2,256,256]{4,3,2,1,0:T(8,128)(2,1)} %arrange_green.1.g_ref), custom_call_target="tpu_custom_call" | custom-call | flops 3221225472 | bytes 12582912 | tf_op jit(solution)/shard_map/collide/pallas_call | solution.py:386
  (1 shorter events, 0.0 us)
Async XLA Ops:
  2.9 57.4 %all-to-all-start.1 = ((f32[32,16,8,128]{3,2,1,0:T(8,128)}), f32[32,16,8,128]{3,2,1,0:T(8,128)S(1)}, u32[]{:S(2)}, u32[]{:S(2)}) async-start(f32[32,16,8,128]{3,2,1,0:T(8,128)} %pack_green.2), calls=%async_computation.1 | async-start | bytes 4194304 | tf_op jit(solution)/shard_map/all_to_all | solution.py:449
  60.2 5.3 %copy-start = (f32[32,16,8,128]{3,2,1,0:T(8,128)}, f32[32,16,8,128]{3,2,1,0:T(8,128)S(1)}, u32[]{:S(2)}) copy-start(f32[32,16,8,128]{3,2,1,0:T(8,128)S(1)} %all-to-all-done.1) | copy-start | bytes 6291460
  60.2 118.9 %all-to-all-start.2 = ((f32[32,16,8,128]{3,2,1,0:T(8,128)}), f32[32,16,8,128]{3,2,1,0:T(8,128)}, u32[]{:S(2)}, u32[]{:S(2)}) async-start(f32[32,16,8,128]{3,2,1,0:T(8,128)} %pack_green.3), calls=%async_computation.2 | async-start | bytes 4194304 | tf_op jit(solution)/shard_map/all_to_all | solution.py:449
  65.5 49.9 %collective-permute-start.5 = (f32[512,256]{1,0:T(8,128)S(1)}, f32[512,256]{1,0:T(8,128)S(1)}, u32[]{:S(2)}, u32[]{:S(2)}) collective-permute-start(f32[512,256]{1,0:T(8,128)S(1)} %get-tuple-element.5), channel_id=1, source_target_pairs={{0,24},{1,25},{2,26},{3,27},{4,28},{5,29},{6,30},{7,31},{8,16},{9,... | collective-permute-start | bytes 1572872 | tf_op jit(solution)/shard_map/ppermute | solution.py:444
  68.1 58.0 %collective-permute-start.3 = (f32[512,256]{1,0:T(8,128)S(1)}, f32[512,256]{1,0:T(8,128)S(1)}, u32[]{:S(2)}, u32[]{:S(2)}) collective-permute-start(f32[512,256]{1,0:T(8,128)S(1)} %get-tuple-element.6), channel_id=1, source_target_pairs={{0,16},{1,17},{2,18},{3,19},{4,20},{5,21},{6,22},{7,23},{8,24},{9,... | collective-permute-start | bytes 1572872 | tf_op jit(solution)/shard_map/ppermute | solution.py:444
  68.6 63.4 %collective-permute-start.1 = (f32[512,256]{1,0:T(8,128)S(1)}, f32[512,256]{1,0:T(8,128)S(1)}, u32[]{:S(2)}, u32[]{:S(2)}) collective-permute-start(f32[512,256]{1,0:T(8,128)S(1)} %get-tuple-element.7), channel_id=1, source_target_pairs={{0,8},{1,9},{2,10},{3,11},{4,12},{5,13},{6,14},{7,15},{8,0},{9,1},... | collective-permute-start | bytes 1572872 | tf_op jit(solution)/shard_map/ppermute | solution.py:444
  69.1 63.6 %collective-permute-start = (f32[512,256]{1,0:T(8,128)S(1)}, f32[512,256]{1,0:T(8,128)S(1)}, u32[]{:S(2)}, u32[]{:S(2)}) collective-permute-start(f32[512,256]{1,0:T(8,128)S(1)} %get-tuple-element.8), channel_id=1, source_target_pairs={{0,1},{1,0},{2,8},{3,9},{4,16},{5,17},{6,24},{7,25},{8,3},{9,2},{1... | collective-permute-start | bytes 1572872 | tf_op jit(solution)/shard_map/ppermute | solution.py:446
  115.4 23.0 %collective-permute-start.6 = (f32[512,256]{1,0:T(8,128)S(1)}, f32[512,256]{1,0:T(8,128)S(1)}, u32[]{:S(2)}, u32[]{:S(2)}) collective-permute-start(f32[512,256]{1,0:T(8,128)S(1)} %collective-permute-done.5), channel_id=1, source_target_pairs={{24,1},{25,0},{26,8},{27,9},{28,16},{29,17},{30,24},{31,25},{16,3}... | collective-permute-start | bytes 1572872 | tf_op jit(solution)/shard_map/ppermute | solution.py:446
  126.1 23.6 %collective-permute-start.4 = (f32[512,256]{1,0:T(8,128)S(1)}, f32[512,256]{1,0:T(8,128)}, u32[]{:S(2)}, u32[]{:S(2)}) collective-permute-start(f32[512,256]{1,0:T(8,128)S(1)} %collective-permute-done.3), channel_id=1, source_target_pairs={{16,1},{17,0},{18,8},{19,9},{20,16},{21,17},{22,24},{23,25},{24,3}... | collective-permute-start | bytes 1572872 | tf_op jit(solution)/shard_map/ppermute | solution.py:446
  132.0 28.8 %collective-permute-start.2 = (f32[512,256]{1,0:T(8,128)S(1)}, f32[512,256]{1,0:T(8,128)}, u32[]{:S(2)}, u32[]{:S(2)}) collective-permute-start(f32[512,256]{1,0:T(8,128)S(1)} %collective-permute-done.1), channel_id=1, source_target_pairs={{8,1},{9,0},{10,8},{11,9},{12,16},{13,17},{14,24},{15,25},{0,3},{1... | collective-permute-start | bytes 1572872 | tf_op jit(solution)/shard_map/ppermute | solution.py:446
  132.7 28.2 %copy-start.1 = (f32[512,256]{1,0:T(8,128)}, f32[512,256]{1,0:T(8,128)S(1)}, u32[]{:S(2)}) copy-start(f32[512,256]{1,0:T(8,128)S(1)} %collective-permute-done.re0_ref) | copy-start | bytes 1572868
  138.4 22.4 %copy-start.2 = (f32[512,256]{1,0:T(8,128)}, f32[512,256]{1,0:T(8,128)S(1)}, u32[]{:S(2)}) copy-start(f32[512,256]{1,0:T(8,128)S(1)} %collective-permute-done.6.im1_ref) | copy-start | bytes 1572868
  179.2 100.8 %all-to-all-start = ((f32[32,2,16,8,128]{4,3,2,1,0:T(8,128)}), f32[32,2,16,8,128]{4,3,2,1,0:T(8,128)}, u32[]{:S(2)}, u32[]{:S(2)}) async-start(f32[32,2,16,8,128]{4,3,2,1,0:T(8,128)} %form_sigma.1), calls=%async_computation | async-start | bytes 8388608 | tf_op jit(solution)/shard_map/all_to_all | solution.py:451

commit v5 on v4

--- a/solution.py
+++ b/solution.py
@@ -191,24 +191,34 @@
 
 
 def send_kernel(x_ref, out_ref):
-    spans = out_ref.shape[1]
-    for v in range(spans):
-        rows = jnp.concatenate([x_ref[0, spans * q + v] for q in range(4)], 0)
-        out_ref[:, v] = rows.T.reshape(out_ref.shape[0], SUBLANES, LANES)
-
-
-def pack_green(x, comp):
+    for v in range(SUBLANES):
+        rows = jnp.concatenate([x_ref[0, q, v] for q in range(4)], 0)
+        out_ref[:, 0, v] = rows.T.reshape(out_ref.shape[0], SUBLANES, LANES)
+
+
+def pack_green(x, start, count):
     _, rows, cols, momenta = x.shape
-    spans = rows * cols // LANES
     devices = momenta // SUBLANES
     parts = momenta // LANES
+    spans = rows * cols // LANES
+    per_part = spans // SUBLANES
+    x = x.reshape(2, 4, spans, cols, momenta)
     return pl.pallas_call(
         send_kernel,
-        grid=(parts,),
-        in_specs=[pl.BlockSpec((1, rows, cols, LANES), lambda p: (comp, 0, 0, p))],
-        out_specs=pl.BlockSpec((devices // parts, spans, SUBLANES, LANES), lambda p: (p, 0, 0, 0)),
-        out_shape=jax.ShapeDtypeStruct((devices, spans, SUBLANES, LANES), f32),
-        cost_estimate=pl.CostEstimate(flops=0, bytes_accessed=x.size * 4, transcendentals=0),
+        grid=(count, parts),
+        in_specs=[
+            pl.BlockSpec(
+                (1, 4, SUBLANES, cols, LANES),
+                lambda n, p: ((n + start) // per_part, 0, (n + start) % per_part, 0, p),
+            )
+        ],
+        out_specs=pl.BlockSpec(
+            (devices // parts, 1, SUBLANES, SUBLANES, LANES), lambda n, p: (p, n, 0, 0, 0)
+        ),
+        out_shape=jax.ShapeDtypeStruct((devices, count, SUBLANES, SUBLANES, LANES), f32),
+        cost_estimate=pl.CostEstimate(
+            flops=0, bytes_accessed=4 * x.size * count // per_part, transcendentals=0
+        ),
         name="pack_green",
     )(x)
 
@@ -319,20 +329,22 @@
     )(flags, x, *others, *tables)
 
 
-def green_kernel(re_ref, im_ref, out_ref, *, rows_count):
+def green_kernel(first_ref, rest_ref, out_ref, *, rows_count):
     cols_count = 2 * rows_count
     k = pl.program_id(0)
     tile_rows = out_ref.shape[3] // rows_count
     step = tile_rows // 4
-    for comp, x_ref in enumerate((re_ref, im_ref)):
+    parts = step // SUBLANES
+    refs = [first_ref.at[:, n] for n in range(first_ref.shape[1])]
+    refs += [rest_ref.at[:, n] for n in range(rest_ref.shape[1])]
+    for comp in range(2):
         for a in range(rows_count):
             for side in range(cols_count // 4):
                 groups = [[] for _ in range(4)]
-                for part in range(step // SUBLANES):
-                    span = pl.ds(SUBLANES * SUBLANES * part + k, SUBLANES, stride=SUBLANES)
-                    loaded = [
-                        x_ref[a * cols_count + 4 * side + n, span, :] for n in range(4)
-                    ]
+                for part in range(parts):
+                    x_ref = refs[parts * comp + part]
+                    span = pl.ds(k, SUBLANES, stride=SUBLANES)
+                    loaded = [x_ref[a * cols_count + 4 * side + n, span, :] for n in range(4)]
                     for q, value in enumerate(regroup(loaded)):
                         groups[q].append(value)
                 for q in range(4):
@@ -344,15 +356,15 @@
 
 
 def arrange_green(parts, rows_count, window):
-    parts = [x.reshape(x.shape[0], -1, LANES) for x in parts]
+    parts = [x.reshape(*x.shape[:2], SUBLANES * SUBLANES, LANES) for x in parts]
     return pl.pallas_call(
         functools.partial(green_kernel, rows_count=rows_count),
         grid=(SUBLANES,),
-        in_specs=[pl.BlockSpec(x.shape, lambda k: (0, 0, 0)) for x in parts],
+        in_specs=[pl.BlockSpec(x.shape, lambda k: (0, 0, 0, 0)) for x in parts],
         out_specs=pl.BlockSpec((1, 2, 2, window, window), lambda k: (k, 0, 0, 0, 0)),
         out_shape=jax.ShapeDtypeStruct((SUBLANES, 2, 2, window, window), bf16),
         cost_estimate=pl.CostEstimate(
-            flops=0, bytes_accessed=4 * parts[0].size * 4, transcendentals=0
+            flops=0, bytes_accessed=8 * sum(x.size for x in parts), transcendentals=0
         ),
         name="arrange_green",
     )(*parts)
@@ -444,9 +456,11 @@
         others[n] = lax.ppermute(others[n], axes, first[n])
     for n in range(4):
         others[n] = lax.ppermute(others[n], axes, second[n])
-    green = [pack_green(x, comp) for comp in range(comps)]
-    for comp in range(comps):
-        green[comp] = lax.all_to_all(green[comp], axes, split_axis=0, concat_axis=0, tiled=True)
+    pieces = comps * tile_rows * tile_cols // (SUBLANES * LANES)
+    early = pieces // 4
+    green = [pack_green(x, 0, early), pack_green(x, early, pieces - early)]
+    for n in range(2):
+        green[n] = lax.all_to_all(green[n], axes, split_axis=0, concat_axis=0, tiled=True)
     sigma = form_sigma(jnp.stack([keep, diagonal]), halves, others, tables)
     sigma = lax.all_to_all(sigma, axes, split_axis=0, concat_axis=0, tiled=True)
     green = arrange_green(green, rows_count, window)

time: 291 us -> 292 us (level)
  waiting for transfers between devices: 209 us -> 172 us
  starting transfers between devices: 31 us -> 62.3 us
  local copies, waits for them, and re-layouts: 1.67 us -> 5.16 us
    all_to_all x2, waiting for transfers between devices: 47.1 us -> 21.6 us  [packed_shards(): lax.all_to_all(green[n], axes, split_axis=0, concat_axis=0, tiled=True)]
    all_to_all x1, starting transfers between devices: 5.9 us -> 29.7 us  [packed_shards(): sigma = lax.all_to_all(sigma, axes, split_axis=0, concat_axis=0, tiled=True)]
    ppermute x4, waiting for transfers between devices: 28.2 us -> 14.9 us  [packed_shards(): others[n] = lax.ppermute(others[n], axes, second[n])]
    ppermute x4, starting transfers between devices: 10.7 us -> 19 us  [packed_shards(): others[n] = lax.ppermute(others[n], axes, second[n])]
  transfers between devices with their start and end apart: 10 -> 10, of which waited for: 7 -> 7; matrix products, arithmetic and copies ran while one was open for 1% -> 1% of each run, Pallas kernels for 12% -> 13%
where the time goes in v5:
time: 292 us; the launch traced here: 291 us
  waiting for transfers between devices  172 us (59%)
  starting transfers between devices  62.3 us (21%)
  Pallas kernels  51.1 us (18%)
  local copies, waits for them, and re-layouts  5.16 us (2%)
    all_to_all x1, waiting for transfers between devices, packed_shards(): sigma = lax.all_to_all(sigma, axes, split_axis=0, concat_axis=0, tiled=True)  81.1 us
    ppermute x3, waiting for transfers between devices, packed_shards(): others[n] = lax.ppermute(others[n], axes, first[n])  54.1 us
    all_to_all x1, starting transfers between devices, packed_shards(): sigma = lax.all_to_all(sigma, axes, split_axis=0, concat_axis=0, tiled=True)  29.7 us
    all_to_all x2, waiting for transfers between devices, packed_shards(): lax.all_to_all(green[n], axes, split_axis=0, concat_axis=0, tiled=True)  21.6 us
    ppermute x4, starting transfers between devices, packed_shards(): others[n] = lax.ppermute(others[n], axes, second[n])  19 us
    pallas_call x1, Pallas kernels, form_sigma(): pl.pallas_call(sigma_kernel, grid_spec=pltpu.PrefetchScalarGridSpec(num_s...  18.3 us
    ppermute x4, waiting for transfers between devices, packed_shards(): others[n] = lax.ppermute(others[n], axes, second[n])  14.9 us
    pallas_call x1, Pallas kernels, arrange_green(): pl.pallas_call(functools.partial(green_kernel, rows_count=rows_count), gr...  13.8 us
  transfers between devices with their start and end apart: 10, of which 7 were waited for; matrix products, arithmetic and copies ran while one was open for 1% of the time, Pallas kernels for 13%

profile of v5, /device:TPU:0, one launch (start us, length us, event | category | flops | bytes accessed | tf_op | source)
XLA Modules:
  0.0 290.9 jit_solution(3464833920394719034)
XLA Ops:
  0.0 2.3 pack_green.2
  2.3 7.3 %all-to-all-start.1 = ((f32[32,1,8,8,128]{4,3,2,1,0:T(8,128)}), f32[32,1,8,8,128]{4,3,2,1,0:T(8,128)S(1)}, u32[]{:S(2)}, u32[]{:S(2)}) async-start(f32[32,1,8,8,128]{4,3,2,1,0:T(8,128)} %pack_green.2), calls=%async_computation.1 | async-start | bytes 2097152 | tf_op jit(solution)/shard_map/all_to_all | solution.py:463
  9.6 5.9 %pack_green.3 = f32[32,3,8,8,128]{4,3,2,1,0:T(8,128)} custom-call(f32[2,4,16,32,256]{4,3,2,1,0:T(8,128)} %bitcast.19), custom_call_target="tpu_custom_call" | custom-call | bytes 6291456 | tf_op jit(solution)/shard_map/pack_green/pallas_call | solution.py:206
  15.5 21.6 %all-to-all-done.1 = f32[32,1,8,8,128]{4,3,2,1,0:T(8,128)S(1)} async-done(((f32[32,1,8,8,128]{4,3,2,1,0:T(8,128)}), f32[32,1,8,8,128]{4,3,2,1,0:T(8,128)S(1)}, u32[]{:S(2)}, u32[]{:S(2)}) %all-to-all-start.1) | async-done | bytes 1048608 | tf_op jit(solution)/shard_map/all_to_all | solution.py:463
  37.1 0.0 copy-start.1
  37.1 1.0 copy-done.1
  38.1 2.8 all-to-all-start.2
  40.9 2.4 dynamic-slice_bitcast_fusion
  43.3 2.6 collective-permute-start.5
  45.9 0.5 collective-permute-start.3
  46.4 0.4 collective-permute-start.1
  46.8 0.0 collective-permute-start
  46.8 42.1 %collective-permute-done.5 = f32[512,256]{1,0:T(8,128)} collective-permute-done((f32[512,256]{1,0:T(8,128)S(1)}, f32[512,256]{1,0:T(8,128)}, u32[]{:S(2)}, u32[]{:S(2)}) %collective-permute-start.5) | collective-permute-done | bytes 524320 | tf_op jit(solution)/shard_map/ppermute | solution.py:456
  88.9 5.1 %collective-permute-start.6 = (f32[512,256]{1,0:T(8,128)}, f32[512,256]{1,0:T(8,128)}, u32[]{:S(2)}, u32[]{:S(2)}) collective-permute-start(f32[512,256]{1,0:T(8,128)} %collective-permute-done.5), channel_id=1, source_target_pairs={{24,1},{25,0},{26,8},{27,9},{28,16},{29,17},{30,24},{31,25},{16,3}... | collective-permute-start | bytes 1572872 | tf_op jit(solution)/shard_map/ppermute | solution.py:458
  94.0 0.6 collective-permute-done.3
  94.6 13.9 %collective-permute-start.4 = (f32[512,256]{1,0:T(8,128)}, f32[512,256]{1,0:T(8,128)}, u32[]{:S(2)}, u32[]{:S(2)}) collective-permute-start(f32[512,256]{1,0:T(8,128)} %collective-permute-done.3), channel_id=1, source_target_pairs={{16,1},{17,0},{18,8},{19,9},{20,16},{21,17},{22,24},{23,25},{24,3}... | collective-permute-start | bytes 1572872 | tf_op jit(solution)/shard_map/ppermute | solution.py:458
  108.5 11.4 %collective-permute-done.1 = f32[512,256]{1,0:T(8,128)} collective-permute-done((f32[512,256]{1,0:T(8,128)S(1)}, f32[512,256]{1,0:T(8,128)}, u32[]{:S(2)}, u32[]{:S(2)}) %collective-permute-start.1) | collective-permute-done | bytes 524320 | tf_op jit(solution)/shard_map/ppermute | solution.py:456
  119.9 0.0 collective-permute-start.2
  119.9 0.6 pad_add_fusion.flags
  120.5 0.0 collective-permute-done.re0_ref
  120.5 0.0 collective-permute-done.6.im1_ref
  120.5 0.9 collective-permute-done.4.im0_ref
  121.5 13.9 %collective-permute-done.2.re1_ref = f32[512,256]{1,0:T(8,128)} collective-permute-done((f32[512,256]{1,0:T(8,128)}, f32[512,256]{1,0:T(8,128)}, u32[]{:S(2)}, u32[]{:S(2)}) %collective-permute-start.2) | collective-permute-done | bytes 524320 | tf_op jit(solution)/shard_map/ppermute | solution.py:458
  135.4 18.3 %form_sigma.1 = f32[32,2,16,8,128]{4,3,2,1,0:T(8,128)} custom-call(s32[2]{0:T(128)} %pad_add_fusion.flags, f32[2,2,1024,256]{3,2,1,0:T(8,128)} %bitcast.21, f32[512,256]{1,0:T(8,128)} %collective-permute-done.re0_ref, f32[512,256]{1,0:T(8,128)} %collective-permute-done.2.re1_ref, f32[512,256]{1,0:T(8,128)} %collective-permute-done.4.im0_ref, ...), custom_call_target="tpu_custom_call" | custom-call | flops 6442450944 | bytes 6291456 | tf_op jit(solution)/shard_map/form_sigma/pallas_call | solution.py:305
  153.8 0.0 all-to-all-done.2
  153.8 0.0 copy-start
  153.8 1.7 copy-done
  155.5 29.7 %all-to-all-start = ((f32[32,2,16,8,128]{4,3,2,1,0:T(8,128)}), f32[32,2,16,8,128]{4,3,2,1,0:T(8,128)}, u32[]{:S(2)}, u32[]{:S(2)}) async-start(f32[32,2,16,8,128]{4,3,2,1,0:T(8,128)} %form_sigma.1), calls=%async_computation | async-start | bytes 8388608 | tf_op jit(solution)/shard_map/all_to_all | solution.py:465
  185.1 13.8 %arrange_green.1.g_ref = bf16[8,2,2,256,256]{4,3,2,1,0:T(8,128)(2,1)} custom-call(f32[32,1,64,128]{3,2,1,0:T(8,128)} %bitcast.23, f32[32,3,64,128]{3,2,1,0:T(8,128)} %bitcast.22), custom_call_target="tpu_custom_call" | custom-call | bytes 8388608 | tf_op jit(solution)/shard_map/arrange_green/pallas_call | solution.py:360
  198.9 81.1 %all-to-all-done = f32[32,2,16,8,128]{4,3,2,1,0:T(8,128)} async-done(((f32[32,2,16,8,128]{4,3,2,1,0:T(8,128)}), f32[32,2,16,8,128]{4,3,2,1,0:T(8,128)}, u32[]{:S(2)}, u32[]{:S(2)}) %all-to-all-start) | async-done | bytes 4194336 | tf_op jit(solution)/shard_map/all_to_all | solution.py:465
  280.1 10.8 %collide.1 = f32[2,8,256,256]{3,2,1,0:T(8,128)} custom-call(f32[32,2,128,128]{3,2,1,0:T(8,128)} %bitcast.9.s_ref, bf16[8,2,2,256,256]{4,3,2,1,0:T(8,128)(2,1)} %arrange_green.1.g_ref), custom_call_target="tpu_custom_call" | custom-call | flops 3221225472 | bytes 12582912 | tf_op jit(solution)/shard_map/collide/pallas_call | solution.py:398
Async XLA Ops:
  2.3 34.8 %all-to-all-start.1 = ((f32[32,1,8,8,128]{4,3,2,1,0:T(8,128)}), f32[32,1,8,8,128]{4,3,2,1,0:T(8,128)S(1)}, u32[]{:S(2)}, u32[]{:S(2)}) async-start(f32[32,1,8,8,128]{4,3,2,1,0:T(8,128)} %pack_green.2), calls=%async_computation.1 | async-start | bytes 2097152 | tf_op jit(solution)/shard_map/all_to_all | solution.py:463
  37.1 1.0 copy-start.1
  38.1 115.7 %all-to-all-start.2 = ((f32[32,3,8,8,128]{4,3,2,1,0:T(8,128)}), f32[32,3,8,8,128]{4,3,2,1,0:T(8,128)S(1)}, u32[]{:S(2)}, u32[]{:S(2)}) async-start(f32[32,3,8,8,128]{4,3,2,1,0:T(8,128)} %pack_green.3), calls=%async_computation.2 | async-start | bytes 6291456 | tf_op jit(solution)/shard_map/all_to_all | solution.py:463
  43.3 45.6 %collective-permute-start.5 = (f32[512,256]{1,0:T(8,128)S(1)}, f32[512,256]{1,0:T(8,128)}, u32[]{:S(2)}, u32[]{:S(2)}) collective-permute-start(f32[512,256]{1,0:T(8,128)S(1)} %get-tuple-element.5), channel_id=1, source_target_pairs={{0,24},{1,25},{2,26},{3,27},{4,28},{5,29},{6,30},{7,31},{8,16},{9,... | collective-permute-start | bytes 1572872 | tf_op jit(solution)/shard_map/ppermute | solution.py:456
  45.9 48.7 %collective-permute-start.3 = (f32[512,256]{1,0:T(8,128)S(1)}, f32[512,256]{1,0:T(8,128)}, u32[]{:S(2)}, u32[]{:S(2)}) collective-permute-start(f32[512,256]{1,0:T(8,128)S(1)} %get-tuple-element.6), channel_id=1, source_target_pairs={{0,16},{1,17},{2,18},{3,19},{4,20},{5,21},{6,22},{7,23},{8,24},{9,... | collective-permute-start | bytes 1572872 | tf_op jit(solution)/shard_map/ppermute | solution.py:456
  46.4 73.5 %collective-permute-start.1 = (f32[512,256]{1,0:T(8,128)S(1)}, f32[512,256]{1,0:T(8,128)}, u32[]{:S(2)}, u32[]{:S(2)}) collective-permute-start(f32[512,256]{1,0:T(8,128)S(1)} %get-tuple-element.7), channel_id=1, source_target_pairs={{0,8},{1,9},{2,10},{3,11},{4,12},{5,13},{6,14},{7,15},{8,0},{9,1},... | collective-permute-start | bytes 1572872 | tf_op jit(solution)/shard_map/ppermute | solution.py:456
  46.8 73.7 %collective-permute-start = (f32[512,256]{1,0:T(8,128)}, f32[512,256]{1,0:T(8,128)}, u32[]{:S(2)}, u32[]{:S(2)}) collective-permute-start(f32[512,256]{1,0:T(8,128)} %get-tuple-element.8), channel_id=1, source_target_pairs={{0,1},{1,0},{2,8},{3,9},{4,16},{5,17},{6,24},{7,25},{8,3},{9,2},{1... | collective-permute-start | bytes 1572872 | tf_op jit(solution)/shard_map/ppermute | solution.py:458
  88.9 31.6 %collective-permute-start.6 = (f32[512,256]{1,0:T(8,128)}, f32[512,256]{1,0:T(8,128)}, u32[]{:S(2)}, u32[]{:S(2)}) collective-permute-start(f32[512,256]{1,0:T(8,128)} %collective-permute-done.5), channel_id=1, source_target_pairs={{24,1},{25,0},{26,8},{27,9},{28,16},{29,17},{30,24},{31,25},{16,3}... | collective-permute-start | bytes 1572872 | tf_op jit(solution)/shard_map/ppermute | solution.py:458
  94.6 26.9 %collective-permute-start.4 = (f32[512,256]{1,0:T(8,128)}, f32[512,256]{1,0:T(8,128)}, u32[]{:S(2)}, u32[]{:S(2)}) collective-permute-start(f32[512,256]{1,0:T(8,128)} %collective-permute-done.3), channel_id=1, source_target_pairs={{16,1},{17,0},{18,8},{19,9},{20,16},{21,17},{22,24},{23,25},{24,3}... | collective-permute-start | bytes 1572872 | tf_op jit(solution)/shard_map/ppermute | solution.py:458
  119.9 15.5 %collective-permute-start.2 = (f32[512,256]{1,0:T(8,128)}, f32[512,256]{1,0:T(8,128)}, u32[]{:S(2)}, u32[]{:S(2)}) collective-permute-start(f32[512,256]{1,0:T(8,128)} %collective-permute-done.1), channel_id=1, source_target_pairs={{8,1},{9,0},{10,8},{11,9},{12,16},{13,17},{14,24},{15,25},{0,3},{1... | collective-permute-start | bytes 1572872 | tf_op jit(solution)/shard_map/ppermute | solution.py:458
  153.8 1.7 copy-start
  155.5 124.6 %all-to-all-start = ((f32[32,2,16,8,128]{4,3,2,1,0:T(8,128)}), f32[32,2,16,8,128]{4,3,2,1,0:T(8,128)}, u32[]{:S(2)}, u32[]{:S(2)}) async-start(f32[32,2,16,8,128]{4,3,2,1,0:T(8,128)} %form_sigma.1), calls=%async_computation | async-start | bytes 8388608 | tf_op jit(solution)/shard_map/all_to_all | solution.py:465

commit v6 on v4

--- a/solution.py
+++ b/solution.py
@@ -277,10 +277,10 @@
             o_im = t_im[:momenta] - t_re[momenta:]
             for w in range(2):
                 lanes = slice(LANES * w, LANES * (w + 1))
-                place = spans * unit + 2 * n + w
+                place = pl.ds(2 * n + w, SUBLANES, stride=spans)
                 shape = (momenta // SUBLANES, SUBLANES, LANES)
-                out_ref[:, 0, place] = o_re[:, lanes].reshape(shape)
-                out_ref[:, 1, place] = o_im[:, lanes].reshape(shape)
+                out_ref[:, 0, unit, place, :] = o_re[:, lanes].reshape(shape)
+                out_ref[:, 1, unit, place, :] = o_im[:, lanes].reshape(shape)
             return carry
 
         lax.fori_loop(0, spans // 2, combine, 0)
@@ -289,7 +289,7 @@
 def form_sigma(flags, x, others, tables):
     comps, _, points, momenta = x.shape
     devices = momenta // SUBLANES
-    spans = 2 * points // LANES
+    out_shape = (devices, comps, 2, SUBLANES * points // LANES, LANES)
     whole = lambda a: pl.BlockSpec(a.shape, lambda n, s: (0,) * a.ndim)
     flops = 3 * 2 * 4 * 2 * (2 * points) * momenta * momenta
     return pl.pallas_call(
@@ -302,15 +302,13 @@
                 *[whole(t) for t in others],
                 *[whole(t) for t in tables],
             ],
-            out_specs=pl.BlockSpec(
-                (devices, comps, spans, SUBLANES, LANES), lambda n, s: (0, 0, 0, 0, 0)
-            ),
+            out_specs=pl.BlockSpec(out_shape, lambda n, s: (0, 0, 0, 0, 0)),
             scratch_shapes=[
                 pltpu.VMEM((2, comps, points, momenta), f32),
                 pltpu.VMEM((2, comps, momenta // LANES, points, LANES), f32),
             ],
         ),
-        out_shape=jax.ShapeDtypeStruct((devices, comps, spans, SUBLANES, LANES), f32),
+        out_shape=jax.ShapeDtypeStruct(out_shape, f32),
         cost_estimate=pl.CostEstimate(
             flops=flops, bytes_accessed=12 * others[0].size * 4, transcendentals=0
         ),
@@ -359,16 +357,15 @@
 
 
 def collide_kernel(s_ref, g_ref, out_ref, left, *, held, blocks):
-    k = pl.program_id(0)
-    edge = out_ref.shape[2] // blocks
+    window = out_ref.shape[2]
+    edge = window // blocks
     for comp in range(2):
         for row in range(blocks):
             for side in range(blocks // 4):
                 loaded = []
                 for n in range(4):
                     source, unit = held[(row, 4 * side + n)]
-                    span = pl.ds(SUBLANES * SUBLANES * unit + k, SUBLANES, stride=SUBLANES)
-                    loaded.append(s_ref[source, comp, span, :])
+                    loaded.append(s_ref[source, comp, unit, 0])
                 high, low = split(jnp.concatenate(regroup(loaded), 0))
                 rows = slice(edge * row, edge * (row + 1))
                 lanes = slice(LANES * side, LANES * (side + 1))
@@ -382,12 +379,13 @@
 
 def collide(sigma, green, held, blocks):
     window = green.shape[-1]
-    sigma = sigma.reshape(sigma.shape[0], 2, -1, LANES)
+    rows = sigma.shape[3] // SUBLANES
+    sigma = sigma.reshape(*sigma.shape[:3], SUBLANES, rows, LANES)
     return pl.pallas_call(
         functools.partial(collide_kernel, held=held, blocks=blocks),
         grid=(SUBLANES,),
         in_specs=[
-            pl.BlockSpec(sigma.shape, lambda k: (0, 0, 0, 0)),
+            pl.BlockSpec((*sigma.shape[:3], 1, rows, LANES), lambda k: (0, 0, 0, k, 0, 0)),
             pl.BlockSpec((1, 2, 2, window, window), lambda k: (k, 0, 0, 0, 0)),
         ],
         out_specs=pl.BlockSpec((2, 1, window, window), lambda k: (0, k, 0, 0)),

time: 291 us -> 291 us (level)
  no operation moved by 1% of the time
where the time goes in v6:
time: 291 us
  waiting for transfers between devices  209 us (72%)
  Pallas kernels  48.6 us (17%)
  starting transfers between devices  31 us (11%)
    all_to_all x1, waiting for transfers between devices, packed_shards(): sigma = lax.all_to_all(sigma, axes, split_axis=0, concat_axis=0, tiled=True)  81.1 us
    ppermute x3, waiting for transfers between devices, packed_shards(): others[n] = lax.ppermute(others[n], axes, first[n])  52.2 us
    all_to_all x2, waiting for transfers between devices, packed_shards(): lax.all_to_all(green[comp], axes, split_axis=0, concat_axis=0, tiled=True)  47.1 us
    ppermute x4, waiting for transfers between devices, packed_shards(): others[n] = lax.ppermute(others[n], axes, second[n])  28.2 us
    pallas_call x1, Pallas kernels, form_sigma(): pl.pallas_call(sigma_kernel, grid_spec=pltpu.PrefetchScalarGridSpec(num_s...  18.6 us
    pallas_call x1, Pallas kernels, arrange_green(): pl.pallas_call(functools.partial(green_kernel, rows_count=rows_count), gr...  13.8 us
    all_to_all x2, starting transfers between devices, packed_shards(): lax.all_to_all(green[comp], axes, split_axis=0, concat_axis=0, tiled=True)  10.9 us
    ppermute x4, starting transfers between devices, packed_shards(): others[n] = lax.ppermute(others[n], axes, second[n])  10.7 us
  transfers between devices with their start and end apart: 10, of which 7 were waited for; matrix products, arithmetic and copies ran while one was open for 1% of the time, Pallas kernels for 12%

profile of v6, /device:TPU:0, one launch (start us, length us, event | category | flops | bytes accessed | tf_op | source)
XLA Modules:
  0.0 290.6 jit_solution(12144653844789069249)
XLA Ops:
  0.0 2.9 pack_green.2
  2.9 7.3 %all-to-all-start.1 = ((f32[32,16,8,128]{3,2,1,0:T(8,128)}), f32[32,16,8,128]{3,2,1,0:T(8,128)S(1)}, u32[]{:S(2)}, u32[]{:S(2)}) async-start(f32[32,16,8,128]{3,2,1,0:T(8,128)} %pack_green.2), calls=%async_computation.1 | async-start | bytes 4194304 | tf_op jit(solution)/shard_map/all_to_all | solution.py:447
  10.2 2.9 %pack_green.3 = f32[32,16,8,128]{3,2,1,0:T(8,128)} custom-call(f32[2,64,32,256]{3,2,1,0:T(8,128)} %bitcast.17), custom_call_target="tpu_custom_call" | custom-call | bytes 4194304 | tf_op jit(solution)/shard_map/pack_green/pallas_call | solution.py:205
  13.1 47.1 %all-to-all-done.1 = f32[32,16,8,128]{3,2,1,0:T(8,128)S(1)} async-done(((f32[32,16,8,128]{3,2,1,0:T(8,128)}), f32[32,16,8,128]{3,2,1,0:T(8,128)S(1)}, u32[]{:S(2)}, u32[]{:S(2)}) %all-to-all-start.1) | async-done | bytes 2097184 | tf_op jit(solution)/shard_map/all_to_all | solution.py:447
  60.2 0.0 copy-start
  60.2 3.6 %all-to-all-start.2 = ((f32[32,16,8,128]{3,2,1,0:T(8,128)}), f32[32,16,8,128]{3,2,1,0:T(8,128)}, u32[]{:S(2)}, u32[]{:S(2)}) async-start(f32[32,16,8,128]{3,2,1,0:T(8,128)} %pack_green.3), calls=%async_computation.2 | async-start | bytes 4194304 | tf_op jit(solution)/shard_map/all_to_all | solution.py:447
  63.9 1.7 dynamic-slice_bitcast_fusion
  65.5 0.0 copy-done
  65.5 2.6 collective-permute-start.5
  68.1 0.5 collective-permute-start.3
  68.6 0.5 collective-permute-start.1
  69.1 0.0 collective-permute-start
  69.1 46.3 %collective-permute-done.5 = f32[512,256]{1,0:T(8,128)S(1)} collective-permute-done((f32[512,256]{1,0:T(8,128)S(1)}, f32[512,256]{1,0:T(8,128)S(1)}, u32[]{:S(2)}, u32[]{:S(2)}) %collective-permute-start.5) | collective-permute-done | bytes 524320 | tf_op jit(solution)/shard_map/ppermute | solution.py:442
  115.4 10.7 %collective-permute-start.6 = (f32[512,256]{1,0:T(8,128)S(1)}, f32[512,256]{1,0:T(8,128)S(1)}, u32[]{:S(2)}, u32[]{:S(2)}) collective-permute-start(f32[512,256]{1,0:T(8,128)S(1)} %collective-permute-done.5), channel_id=1, source_target_pairs={{24,1},{25,0},{26,8},{27,9},{28,16},{29,17},{30,24},{31,25},{16,3}... | collective-permute-start | bytes 1572872 | tf_op jit(solution)/shard_map/ppermute | solution.py:444
  126.1 0.0 collective-permute-done.3
  126.1 0.0 collective-permute-start.4
  126.1 5.9 %collective-permute-done.1 = f32[512,256]{1,0:T(8,128)S(1)} collective-permute-done((f32[512,256]{1,0:T(8,128)S(1)}, f32[512,256]{1,0:T(8,128)S(1)}, u32[]{:S(2)}, u32[]{:S(2)}) %collective-permute-start.1) | collective-permute-done | bytes 524320 | tf_op jit(solution)/shard_map/ppermute | solution.py:442
  132.0 0.0 collective-permute-start.2
  132.0 0.7 pad_add_fusion.flags
  132.7 0.0 collective-permute-done.re0_ref
  132.7 0.0 copy-start.1
  132.7 5.8 %collective-permute-done.6.im1_ref = f32[512,256]{1,0:T(8,128)S(1)} collective-permute-done((f32[512,256]{1,0:T(8,128)S(1)}, f32[512,256]{1,0:T(8,128)S(1)}, u32[]{:S(2)}, u32[]{:S(2)}) %collective-permute-start.6) | collective-permute-done | bytes 524320 | tf_op jit(solution)/shard_map/ppermute | solution.py:444
  138.4 11.2 %collective-permute-done.4.im0_ref = f32[512,256]{1,0:T(8,128)} collective-permute-done((f32[512,256]{1,0:T(8,128)S(1)}, f32[512,256]{1,0:T(8,128)}, u32[]{:S(2)}, u32[]{:S(2)}) %collective-permute-start.4) | collective-permute-done | bytes 524320 | tf_op jit(solution)/shard_map/ppermute | solution.py:444
  149.7 11.2 %collective-permute-done.2.re1_ref = f32[512,256]{1,0:T(8,128)} collective-permute-done((f32[512,256]{1,0:T(8,128)S(1)}, f32[512,256]{1,0:T(8,128)}, u32[]{:S(2)}, u32[]{:S(2)}) %collective-permute-start.2) | collective-permute-done | bytes 524320 | tf_op jit(solution)/shard_map/ppermute | solution.py:444
  160.8 0.0 copy-done.1
  160.8 0.0 copy-done.2
  160.8 18.6 %form_sigma.1 = f32[32,2,2,64,128]{4,3,2,1,0:T(8,128)} custom-call(s32[2]{0:T(128)} %pad_add_fusion.flags, f32[2,2,1024,256]{3,2,1,0:T(8,128)} %bitcast.19, f32[512,256]{1,0:T(8,128)} %copy-done.1, f32[512,256]{1,0:T(8,128)} %collective-permute-done.2.re1_ref, f32[512,256]{1,0:T(8,128)} %collective-permute-done.4.im0_ref, f32[512,256]{1,0:T(8,128)} %copy-done.2, ...), custom_call_target="tpu_custom_call" | custom-call | flops 6442450944 | bytes 6291456 | tf_op jit(solution)/shard_map/form_sigma/pallas_call | solution.py:295
  179.5 0.0 all-to-all-done.2
  179.5 5.9 %all-to-all-start = ((f32[32,2,2,64,128]{4,3,2,1,0:T(8,128)}), f32[32,2,2,64,128]{4,3,2,1,0:T(8,128)}, u32[]{:S(2)}, u32[]{:S(2)}) async-start(f32[32,2,2,64,128]{4,3,2,1,0:T(8,128)} %form_sigma.1), calls=%async_computation | async-start | bytes 8388608 | tf_op jit(solution)/shard_map/all_to_all | solution.py:449
  185.4 13.8 %arrange_green.1.g_ref = bf16[8,2,2,256,256]{4,3,2,1,0:T(8,128)(2,1)} custom-call(f32[32,128,128]{2,1,0:T(8,128)} %bitcast.20, f32[32,128,128]{2,1,0:T(8,128)} %bitcast.11.im_ref), custom_call_target="tpu_custom_call" | custom-call | bytes 8388608 | tf_op jit(solution)/shard_map/arrange_green/pallas_call | solution.py:346
  199.2 81.1 %all-to-all-done = f32[32,2,2,64,128]{4,3,2,1,0:T(8,128)} async-done(((f32[32,2,2,64,128]{4,3,2,1,0:T(8,128)}), f32[32,2,2,64,128]{4,3,2,1,0:T(8,128)}, u32[]{:S(2)}, u32[]{:S(2)}) %all-to-all-start) | async-done | bytes 4194336 | tf_op jit(solution)/shard_map/all_to_all | solution.py:449
  280.3 10.3 %collide.1 = f32[2,8,256,256]{3,2,1,0:T(8,128)} custom-call(f32[32,2,2,8,8,128]{5,4,3,2,1,0:T(8,128)} %bitcast.9.s_ref, bf16[8,2,2,256,256]{4,3,2,1,0:T(8,128)(2,1)} %arrange_green.1.g_ref), custom_call_target="tpu_custom_call" | custom-call | flops 3221225472 | bytes 12582912 | tf_op jit(solution)/shard_map/collide/pallas_call | solution.py:384
  (1 shorter events, 0.0 us)
Async XLA Ops:
  2.9 57.4 %all-to-all-start.1 = ((f32[32,16,8,128]{3,2,1,0:T(8,128)}), f32[32,16,8,128]{3,2,1,0:T(8,128)S(1)}, u32[]{:S(2)}, u32[]{:S(2)}) async-start(f32[32,16,8,128]{3,2,1,0:T(8,128)} %pack_green.2), calls=%async_computation.1 | async-start | bytes 4194304 | tf_op jit(solution)/shard_map/all_to_all | solution.py:447
  60.2 5.3 %copy-start = (f32[32,16,8,128]{3,2,1,0:T(8,128)}, f32[32,16,8,128]{3,2,1,0:T(8,128)S(1)}, u32[]{:S(2)}) copy-start(f32[32,16,8,128]{3,2,1,0:T(8,128)S(1)} %all-to-all-done.1) | copy-start | bytes 6291460
  60.2 119.2 %all-to-all-start.2 = ((f32[32,16,8,128]{3,2,1,0:T(8,128)}), f32[32,16,8,128]{3,2,1,0:T(8,128)}, u32[]{:S(2)}, u32[]{:S(2)}) async-start(f32[32,16,8,128]{3,2,1,0:T(8,128)} %pack_green.3), calls=%async_computation.2 | async-start | bytes 4194304 | tf_op jit(solution)/shard_map/all_to_all | solution.py:447
  65.5 49.9 %collective-permute-start.5 = (f32[512,256]{1,0:T(8,128)S(1)}, f32[512,256]{1,0:T(8,128)S(1)}, u32[]{:S(2)}, u32[]{:S(2)}) collective-permute-start(f32[512,256]{1,0:T(8,128)S(1)} %get-tuple-element.5), channel_id=1, source_target_pairs={{0,24},{1,25},{2,26},{3,27},{4,28},{5,29},{6,30},{7,31},{8,16},{9,... | collective-permute-start | bytes 1572872 | tf_op jit(solution)/shard_map/ppermute | solution.py:442
  68.1 58.0 %collective-permute-start.3 = (f32[512,256]{1,0:T(8,128)S(1)}, f32[512,256]{1,0:T(8,128)S(1)}, u32[]{:S(2)}, u32[]{:S(2)}) collective-permute-start(f32[512,256]{1,0:T(8,128)S(1)} %get-tuple-element.6), channel_id=1, source_target_pairs={{0,16},{1,17},{2,18},{3,19},{4,20},{5,21},{6,22},{7,23},{8,24},{9,... | collective-permute-start | bytes 1572872 | tf_op jit(solution)/shard_map/ppermute | solution.py:442
  68.6 63.4 %collective-permute-start.1 = (f32[512,256]{1,0:T(8,128)S(1)}, f32[512,256]{1,0:T(8,128)S(1)}, u32[]{:S(2)}, u32[]{:S(2)}) collective-permute-start(f32[512,256]{1,0:T(8,128)S(1)} %get-tuple-element.7), channel_id=1, source_target_pairs={{0,8},{1,9},{2,10},{3,11},{4,12},{5,13},{6,14},{7,15},{8,0},{9,1},... | collective-permute-start | bytes 1572872 | tf_op jit(solution)/shard_map/ppermute | solution.py:442
  69.1 63.6 %collective-permute-start = (f32[512,256]{1,0:T(8,128)S(1)}, f32[512,256]{1,0:T(8,128)S(1)}, u32[]{:S(2)}, u32[]{:S(2)}) collective-permute-start(f32[512,256]{1,0:T(8,128)S(1)} %get-tuple-element.8), channel_id=1, source_target_pairs={{0,1},{1,0},{2,8},{3,9},{4,16},{5,17},{6,24},{7,25},{8,3},{9,2},{1... | collective-permute-start | bytes 1572872 | tf_op jit(solution)/shard_map/ppermute | solution.py:444
  115.4 23.0 %collective-permute-start.6 = (f32[512,256]{1,0:T(8,128)S(1)}, f32[512,256]{1,0:T(8,128)S(1)}, u32[]{:S(2)}, u32[]{:S(2)}) collective-permute-start(f32[512,256]{1,0:T(8,128)S(1)} %collective-permute-done.5), channel_id=1, source_target_pairs={{24,1},{25,0},{26,8},{27,9},{28,16},{29,17},{30,24},{31,25},{16,3}... | collective-permute-start | bytes 1572872 | tf_op jit(solution)/shard_map/ppermute | solution.py:444
  126.1 23.6 %collective-permute-start.4 = (f32[512,256]{1,0:T(8,128)S(1)}, f32[512,256]{1,0:T(8,128)}, u32[]{:S(2)}, u32[]{:S(2)}) collective-permute-start(f32[512,256]{1,0:T(8,128)S(1)} %collective-permute-done.3), channel_id=1, source_target_pairs={{16,1},{17,0},{18,8},{19,9},{20,16},{21,17},{22,24},{23,25},{24,3}... | collective-permute-start | bytes 1572872 | tf_op jit(solution)/shard_map/ppermute | solution.py:444
  132.0 28.8 %collective-permute-start.2 = (f32[512,256]{1,0:T(8,128)S(1)}, f32[512,256]{1,0:T(8,128)}, u32[]{:S(2)}, u32[]{:S(2)}) collective-permute-start(f32[512,256]{1,0:T(8,128)S(1)} %collective-permute-done.1), channel_id=1, source_target_pairs={{8,1},{9,0},{10,8},{11,9},{12,16},{13,17},{14,24},{15,25},{0,3},{1... | collective-permute-start | bytes 1572872 | tf_op jit(solution)/shard_map/ppermute | solution.py:444
  132.7 28.2 %copy-start.1 = (f32[512,256]{1,0:T(8,128)}, f32[512,256]{1,0:T(8,128)S(1)}, u32[]{:S(2)}) copy-start(f32[512,256]{1,0:T(8,128)S(1)} %collective-permute-done.re0_ref) | copy-start | bytes 1572868
  138.4 22.4 %copy-start.2 = (f32[512,256]{1,0:T(8,128)}, f32[512,256]{1,0:T(8,128)S(1)}, u32[]{:S(2)}) copy-start(f32[512,256]{1,0:T(8,128)S(1)} %collective-permute-done.6.im1_ref) | copy-start | bytes 1572868
  179.5 100.8 %all-to-all-start = ((f32[32,2,2,64,128]{4,3,2,1,0:T(8,128)}), f32[32,2,2,64,128]{4,3,2,1,0:T(8,128)}, u32[]{:S(2)}, u32[]{:S(2)}) async-start(f32[32,2,2,64,128]{4,3,2,1,0:T(8,128)} %form_sigma.1), calls=%async_computation | async-start | bytes 8388608 | tf_op jit(solution)/shard_map/all_to_all | solution.py:449
